TPU v7x, 32 devices: a whole 2x2x4 slice. The times are simulated.
32 devices in a mesh: wide: 8 (over z, y), narrow: 4 (over x, core).
Axes of the slice: x: 2, y: 2, z: 4, core: 2. Of those that a mesh axis runs over, the one named last changes fastest.
Arguments:
- tokens: bfloat16 [4096, 768], P('wide'), may hold values from -6 to 6
- store: bfloat16 [8, 1664, 768], P('wide', 'narrow'), may hold values from -6 to 6
- summary_length: int32 [8], P('wide'), may hold values from 64 to 512, as said below
- top_index: int32 [4096, 12, 4, 256], P('wide', 'narrow'), may hold values from 0 to 415, as said below
- cotangent: bfloat16 [4096, 768], P('wide'), may hold values from -6 to 6
- self_qkv_weight: bfloat16 [3, 768, 768], P(None, None, 'narrow'), may hold values from -0.21875 to 0.21875
- self_qv_bias: float32 [2, 768], P(None, 'narrow'), may hold values from -3 to 3
- self_out_weight: bfloat16 [768, 768], P('narrow'), may hold values from -0.875 to 0.875
- self_out_bias: float32 [768], replicated, may hold values from -3 to 3
- qkv_weight: bfloat16 [3, 768, 768], P(None, None, 'narrow'), may hold values from -0.21875 to 0.21875
- qv_bias: float32 [2, 768], P(None, 'narrow'), may hold values from -3 to 3
- out_weight: bfloat16 [768, 768], P('narrow'), may hold values from -0.875 to 0.875
- out_bias: float32 [768], replicated, may hold values from -3 to 3
- fc1_weight: bfloat16 [768, 3072], P(None, 'narrow'), may hold values from -0.21875 to 0.21875
- fc1_bias: float32 [3072], P('narrow'), may hold values from -3 to 3
- fc2_weight: bfloat16 [3072, 768], P('narrow'), may hold values from -0.109375 to 0.109375
- fc2_bias: float32 [768], replicated, may hold values from -3 to 3
- norm_gain: float32 [3, 768], replicated, may hold values from 0.4 to 1.6
- norm_shift: float32 [3, 768], replicated, may hold values from -2 to 2
Outputs:
- mixed: bfloat16 [4096, 768], P('wide')
- tokens_grad: float32 [4096, 768], P('wide')
- store_grad: float32 [8, 1664, 768], P('wide', 'narrow')
- self_qkv_grad: float32 [3, 768, 768], P(None, 'wide', 'narrow')
- self_qv_bias_grad: float32 [2, 768], P(None, 'narrow')
- self_out_weight_grad: float32 [768, 768], P('narrow', 'wide')
- self_out_bias_grad: float32 [768], replicated
- qkv_grad: float32 [3, 768, 768], P(None, 'wide', 'narrow')
- qv_bias_grad: float32 [2, 768], P(None, 'narrow')
- out_weight_grad: float32 [768, 768], P('narrow', 'wide')
- out_bias_grad: float32 [768], replicated
- fc1_grad: float32 [768, 3072], P('wide', 'narrow')
- fc1_bias_grad: float32 [3072], P('narrow')
- fc2_grad: float32 [3072, 768], P('narrow', 'wide')
- fc2_bias_grad: float32 [768], replicated
- norm_gain_grad: float32 [3, 768], replicated
- norm_shift_grad: float32 [3, 768], replicated
Inputs may be any that keep to these rules, and one draw needn't show every extreme that they name: `summary_length`: the longest summary has exactly 512 tokens and the shortest exactly 64. `top_index`: each list of 256 indices is strictly increasing, starts at 0 and ends at 415.
All inputs are finite; a program needn't handle non-finite values.
Results may differ from a plain program's by a relative error of at most 0.025.
Values may be sent and summed in bfloat16 or wider, within the bound.
No kernel may reach another device: no remote copies, remote signals or barrier semaphores. Data moves between devices by JAX's collectives and lax.ppermute only.
A program may use at most 128 MiB of HBM per device.

v0:
```python
import functools

import jax
import jax.numpy as jnp
from jax import lax
from jax.experimental import pallas as pl
from jax.experimental.pallas import tpu as pltpu
from jax.sharding import PartitionSpec as P

F32 = jnp.float32
BF = jnp.bfloat16
NN = (((1,), (0,)), ((), ()))
NT = (((1,), (1,)), ((), ()))
TN = (((0,), (0,)), ((), ()))
EPS = 1e-05
PACE = 1.1e8
SELF_MIB = 60
EXTRA = 16

CORE = [(i, i ^ 1) for i in range(4)]
ACROSS = [(i, i ^ 2) for i in range(4)]


def mm(left, right, dims=NN):
    return lax.dot_general(left, right, dims, preferred_element_type=F32)


def shape(*dims, dtype=F32):
    return jax.ShapeDtypeStruct(dims, dtype)


def tie(value, *earlier):
    return lax.optimization_barrier((value, *earlier))[0]


class Operand:
    def __init__(self, source, buffer, sems, first, parts):
        self.buffer = buffer
        self.parts = parts
        if parts:
            self.copies = [
                pltpu.make_async_copy(source.at[i], buffer.at[i], sems.at[first + i]) for i in range(buffer.shape[0])
            ]
        else:
            self.copies = [pltpu.make_async_copy(source, buffer, sems.at[first])]
        self.waited = [False] * len(self.copies)
        for copy in self.copies:
            copy.start()

    def ready(self, part=None):
        for i, copy in enumerate(self.copies):
            if not self.waited[i] and (part is None or i == part):
                copy.wait()
                self.waited[i] = True

    @property
    def shape(self):
        return self.buffer.shape

    def __getitem__(self, at):
        self.ready(at if self.parts and isinstance(at, int) else None)
        return self.buffer[at]


class Result:
    def __init__(self, target, buffer, sems, first, parts):
        self.buffer = buffer
        if parts:
            self.copies = [
                pltpu.make_async_copy(buffer.at[i], target.at[i], sems.at[first + i]) for i in range(buffer.shape[0])
            ]
        else:
            self.copies = [pltpu.make_async_copy(buffer, target, sems.at[first])]
        self.started = [False] * len(self.copies)

    @property
    def shape(self):
        return self.buffer.shape

    @property
    def dtype(self):
        return self.buffer.dtype

    def __setitem__(self, at, value):
        self.buffer[at] = value

    def flush(self, part=0):
        self.copies[part].start()
        self.started[part] = True

    def finish(self):
        for i in range(len(self.copies)):
            if not self.started[i]:
                self.flush(i)
        for copy in self.copies:
            copy.wait()


def far(array, take=None, dims=None, parts=False):
    return ("far", array, take, tuple(dims or array.shape), parts)


def near(array, take=None):
    return ("near", array, take, None, False)


def raw(array):
    return ("raw", array, None, None, False)


def launch(body, name, at, ins, outs, scratch=(), mib=16, us=2.0):
    in_specs = [pl.BlockSpec(memory_space=pltpu.SMEM)]
    buffers, n_in, n_out = [], 0, 0
    for kind, array, _, dims, parts in ins:
        in_specs.append(pl.BlockSpec(memory_space=pltpu.VMEM if kind == "near" else pltpu.HBM))
        if kind == "far":
            buffers.append(pltpu.VMEM(dims, array.dtype))
            n_in += dims[0] if parts else 1
    out_specs, structs = [], []
    for out in outs:
        if isinstance(out, tuple):
            struct, parts = out
            out_specs.append(pl.BlockSpec(memory_space=pltpu.HBM))
            buffers.append(pltpu.VMEM(struct.shape, struct.dtype))
            n_out += struct.shape[0] if parts else 1
        else:
            struct = out
            out_specs.append(pl.BlockSpec(memory_space=pltpu.VMEM))
        structs.append(struct)
    n_buffers = len(buffers)
    sems = [pltpu.SemaphoreType.DMA((max(n, 1),)) for n in (n_in, n_out)]

    def kernel(at_ref, *refs):
        in_refs, out_refs = refs[: len(ins)], refs[len(ins) : len(ins) + len(outs)]
        rest = refs[len(ins) + len(outs) :]
        bufs, user, (in_sems, out_sems) = list(rest[:n_buffers]), rest[n_buffers:-2], rest[-2:]
        place, given = 0, []
        for ref, (kind, _, take, dims, parts) in zip(in_refs, ins):
            source = take(ref, at_ref) if take else ref
            if kind == "far":
                given.append(Operand(source, bufs.pop(0), in_sems, place, parts))
                place += dims[0] if parts else 1
            else:
                given.append(source)
        place, results = 0, []
        for ref, out in zip(out_refs, outs):
            if isinstance(out, tuple):
                results.append(Result(ref, bufs.pop(0), out_sems, place, out[1]))
                place += out[0].shape[0] if out[1] else 1
            else:
                results.append(ref)
        body(at_ref, given, results, user)
        for operand in given:
            if isinstance(operand, Operand):
                operand.ready()
        for result in results:
            if isinstance(result, Result):
                result.finish()

    return pl.pallas_call(
        kernel,
        in_specs=in_specs,
        out_specs=out_specs,
        out_shape=structs,
        scratch_shapes=buffers + list(scratch) + sems,
        compiler_params=pltpu.CompilerParams(vmem_limit_bytes=mib << 20),
        cost_estimate=pl.CostEstimate(flops=int(us * PACE), bytes_accessed=1000, transcendentals=0),
        name=name,
    )(at, *[entry[1] for entry in ins])


def norm_stats(value):
    centre = value - jnp.mean(value, axis=-1, keepdims=True)
    spread = jnp.mean(centre * centre, axis=-1, keepdims=True)
    inverse = lax.rsqrt(spread + EPS)
    return centre * inverse, inverse


def norm_backward(grad, normed, inverse, gain):
    scaled = grad * gain
    centred = scaled - jnp.mean(scaled, axis=-1, keepdims=True)
    return inverse * (centred - normed * jnp.mean(scaled * normed, axis=-1, keepdims=True))


def column_sum(value):
    return jnp.sum(value, axis=0, keepdims=True)


def erf(value):
    x = jnp.clip(value, -4.0, 4.0)
    y = x * x
    top = jnp.full_like(y, -2.72614225801306e-10)
    for factor in (
        2.77068142495902e-08,
        -2.10102402082508e-06,
        -5.69250639462346e-05,
        -7.34990630326855e-04,
        -2.95459980854025e-03,
        -1.60960333262415e-02,
    ):
        top = top * y + factor
    low = jnp.full_like(y, -1.45660718464996e-05)
    for factor in (
        -2.13374055278905e-04,
        -1.68282697438203e-03,
        -7.37332916720468e-03,
        -1.42647390514189e-02,
    ):
        low = low * y + factor
    return x * top / low


def gelu_pair(pre):
    phi = 0.5 * (1.0 + erf(pre * 0.7071067811865476))
    return (pre * phi).astype(BF), phi + pre * (jnp.exp(pre * pre * -0.5) * 0.3989422804014327)


def three_terms(value):
    high = value.astype(BF)
    rest = value - high.astype(F32)
    middle = rest.astype(BF)
    return jnp.concatenate([high, middle, (rest - middle.astype(F32)).astype(BF)], axis=0)


def from_terms(stacked):
    rows = stacked.shape[0] // 3
    terms = stacked.astype(F32)
    return terms[:rows] + terms[rows : 2 * rows] + terms[2 * rows :]


def rows_at(place, rows):
    return pl.ds(pl.multiple_of(place * rows, rows), rows)


def self_forward(at, tokens, w, b, wo, b1, nh):
    rows, width = tokens.shape
    local = w.shape[1]
    half = rows // 2
    hd = local // nh
    scale = hd**-0.5

    def body(at, ins, outs, _):
        tok, w, wo, b, b1 = ins
        qkv, prob, flat, send, keep = outs
        x = tok[...]
        q = (mm(x, w[0], NT) + b[0:1]).astype(BF)
        k = mm(x, w[1], NT).astype(BF)
        v = (mm(x, w[2], NT) + b[1:2]).astype(BF)
        for i, value in enumerate((q, k, v)):
            qkv[i] = value
            qkv.flush(i)
        row_ids = lax.broadcasted_iota(jnp.int32, (rows, rows), 0)
        key_ids = lax.broadcasted_iota(jnp.int32, (rows, rows), 1)
        allowed = (key_ids <= row_ids) & (key_ids < at[3])
        found = []
        for h in range(nh):
            part = slice(h * hd, (h + 1) * hd)
            scores = mm(q[:, part], k[:, part], NT) * scale
            scores = jnp.where(allowed, scores, -1e30)
            shifted = jnp.exp(scores - jnp.max(scores, axis=1, keepdims=True))
            weights = (shifted * (1.0 / jnp.sum(shifted, axis=1, keepdims=True))).astype(BF)
            prob[h] = weights
            prob.flush(h)
            found.append(mm(weights, v[:, part]).astype(BF))
        flat[...] = jnp.concatenate(found, axis=1)
        flat.flush()
        send[0:half, :] = mm(flat.buffer[rows_at(1 - at[0], half), :], wo[...]).astype(BF)
        send[half:, :] = jnp.concatenate([three_terms(b1[...]), jnp.zeros((16 - 3, width), BF)], axis=0)
        send.flush()
        keep[...] = mm(flat.buffer[rows_at(at[0], half), :], wo[...])

    return launch(
        body,
        "self_fwd",
        at,
        [far(tokens), far(w, parts=True), far(wo), far(b), far(b1)],
        [
            (shape(3, rows, local, dtype=BF), True),
            (shape(nh, rows, rows, dtype=BF), True),
            (shape(rows, local, dtype=BF), False),
            (shape(half + 16, width, dtype=BF), False),
            (shape(half, width), False),
        ],
        mib=SELF_MIB,
        us=4,
    )


def first_norm(at, mine, other, tokens, bias, gain, shift):
    half, width = mine.shape[0] - 16, mine.shape[1]

    def body(at, ins, outs, _):
        mine, other, tok, bias, gain, shift = ins
        total, after, low = outs
        value = tok[...].astype(F32) + (mine[0:half].astype(F32) + other[0:half].astype(F32)) + bias[...]
        total[...] = value
        normed, _ = norm_stats(value)
        result = normed * gain[0:1] + shift[0:1]
        after[...] = result
        low[...] = result.astype(BF)

    return launch(
        body,
        "first_norm",
        at,
        [
            near(mine),
            near(other),
            near(tokens, lambda ref, at: ref.at[rows_at(at[0], half), :]),
            near(bias),
            near(gain),
            near(shift),
        ],
        [shape(half, width), shape(half, width), shape(half, width, dtype=BF)],
        us=1.7,
    )


def index_rows(top_index):
    rows, nh, ns, keep = top_index.shape
    flat = top_index.reshape(rows, nh, ns, keep // 128, 128).transpose(0, 1, 3, 2, 4)
    return flat.reshape(rows * nh * ns * (keep // 128), 128)


def make_mask(at, flat, dims, seg, tile, turn):
    rows, nh, ns, keep = dims
    halves = keep // 128
    per_row = nh * ns * halves
    tiles = rows // 2 // tile
    columns = ns * seg
    blocks = columns // 128
    group = 32

    def body(at, ins, outs, _):
        (index,) = ins
        (bias,) = outs
        lane = lax.broadcasted_iota(jnp.int32, (group, 128), 1).astype(F32)
        lane_low = lane.astype(BF)
        empty = jnp.full((group, 128), -1.0, BF)
        own = at[2]
        steps = []
        step = 1
        while step <= seg - keep:
            steps.insert(0, step)
            step *= 2
        turns = steps + [(seg * s) % 128 for s in range(ns)]
        below = {s: lane_low < jnp.asarray(s, BF) for s in turns if 0 < s < 128}

        for t in range(tiles):
            index.ready(t)
            source = index.buffer.at[t]

            def one_group(g, _):
                for h in range(nh):
                    v = [empty] * blocks
                    for slot in range(ns):
                        first, turn = divmod(seg * slot, 128)
                        for c in range(halves):
                            start = g * (group * per_row) + h * ns * halves + c * ns + (own ^ slot)
                            found = jnp.concatenate(
                                [source[pl.ds(start + q * 8 * per_row, 8, stride=per_row), :] for q in range(group // 8)],
                                axis=0,
                            )
                            ahead = (found.astype(F32) - (lane + float(128 * c))).astype(BF)
                            at_block = first + c
                            if turn == 0:
                                v[at_block] = ahead
                            else:
                                turned = pltpu.roll(ahead, turn, axis=1)
                                v[at_block] = jnp.where(below[turn], v[at_block], turned)
                                v[at_block + 1] = jnp.where(below[turn], turned, v[at_block + 1])
                    for s in steps:
                        gap = jnp.asarray(s, BF)
                        moved = [x - gap for x in v]
                        stay = [jnp.where(x >= gap, empty, x) for x in v]
                        if s % 128 == 0:
                            hop = s // 128
                            v = stay[:hop] + [jnp.maximum(stay[i], moved[i - hop]) for i in range(hop, blocks)]
                        else:
                            turned = [pltpu.roll(x, s, axis=1) for x in moved]
                            v = [
                                jnp.maximum(stay[i], jnp.where(below[s], turned[i - 1], turned[i])) for i in range(blocks)
                            ]
                    for i in range(blocks):
                        bias[h, pl.ds(pl.multiple_of(t * tile + g * group, group), group), i * 128 : (i + 1) * 128] = v[
                            i
                        ] * jnp.asarray(1e30, BF)
                return 0

            lax.fori_loop(0, tile // group, one_group, 0)

    flat = flat.reshape(2 * tiles, tile * per_row, 128)
    return launch(
        body,
        "mask",
        at,
        [
            far(
                flat,
                lambda ref, at: ref.at[pl.ds((at[0] ^ turn) * tiles, tiles)],
                (tiles, tile * per_row, 128),
                parts=True,
            )
        ],
        [shape(nh, rows // 2, columns, dtype=BF)],
        us=10,
    )[0]


def keys_values(at, shards, w, nh):
    seg, width = shards[0].shape
    local = w.shape[1]
    hd = local // nh

    def body(at, ins, outs, _):
        for slot in range(4):
            x = ins[slot][...]
            span = slice(slot * seg, (slot + 1) * seg)
            for i, out in enumerate(outs):
                full = mm(x, ins[4][i + 1], NT)
                high = full.astype(BF)
                low = (full - high.astype(F32)).astype(BF)
                for h in range(nh):
                    part = slice(h * hd, (h + 1) * hd)
                    out[h, span, :] = jnp.concatenate([high[:, part], low[:, part]], axis=1)

    out = shape(nh, 4 * seg, 2 * hd, dtype=BF)
    return launch(body, "keys_values", at, [near(s) for s in shards] + [near(w)], [out, out], us=2)


def cross_forward(at, mine, other, bias_mine, bias_other, keys, values, w, b, wo, nh):
    half, width = mine.shape
    rows = 2 * half
    local = w.shape[1]
    hd = local // nh
    slots = keys.shape[1]
    scale = hd**-0.5

    def body(at, ins, outs, scratch):
        mine, other, wq, keys, bias_mine, bias_other, values, wo, b = ins
        keep, send, raised, inverse, query, heads = outs
        twice, found = scratch
        for r, x in enumerate((mine, other)):
            q = (mm(x[...], wq[0], NT) + b[0:1]).astype(BF)
            query[r * half : (r + 1) * half, :] = q
            scaled = q * jnp.asarray(scale, BF)
            for h in range(nh):
                part = scaled[:, h * hd : (h + 1) * hd]
                twice[h, r * half : (r + 1) * half, :] = jnp.concatenate([part, part], axis=1)

        def one_head(h, _):
            for r, bias in enumerate((bias_mine, bias_other)):
                span = slice(r * half, (r + 1) * half)
                scores = mm(twice[h, span, :], keys[h], NT) + bias[h].astype(F32)
                e = jnp.exp(scores - jnp.max(scores, axis=1, keepdims=True))
                total = 1.0 / jnp.sum(e, axis=1, keepdims=True)
                low = e.astype(BF)
                raised[h, span, :] = low
                inverse[h, span, :] = jnp.broadcast_to(total, (half, 128))
                both = mm(low, values[h])
                found[h, span, :] = (both[:, :hd] + both[:, hd:]) * total
            return 0

        lax.fori_loop(0, nh, one_head, 0)
        for r, target in enumerate((keep, send)):
            span = slice(r * half, (r + 1) * half)
            out = (jnp.concatenate([found[h, span, :] for h in range(nh)], axis=1) + b[1:2]).astype(BF)
            heads[span, :] = out
            target[...] = mm(out, wo[...]).astype(target.dtype)

    return launch(
        body,
        "cross_fwd",
        at,
        [near(a) for a in (mine, other, w, keys, bias_mine, bias_other, values, wo, b)],
        [
            shape(half, width),
            shape(half, width, dtype=BF),
            shape(nh, rows, slots, dtype=BF),
            shape(nh, rows, 128),
            shape(rows, local, dtype=BF),
            shape(rows, local, dtype=BF),
        ],
        scratch=[pltpu.VMEM((nh, rows, 2 * hd), BF), pltpu.VMEM((nh, rows, hd), F32)],
        mib=30,
        us=9,
    )


def feed(at, after, kept, close, distant, cot, weights, b1, terms, out_bias, fc2_bias, gain, shift):
    rows, width = distant.shape
    units = weights[0][0].shape[1]
    base = terms[0].shape[0] - 16

    def body(at, ins, outs, scratch):
        after, kept, close, distant, cot, out_bias, fc2_bias, gain, shift, b1, close_terms, far_terms = ins[:12]
        f1, f2, slope, sems = scratch
        copies = []
        for matrix, target in enumerate((f1, f2)):
            own, core, *halves = ins[12 + 6 * matrix : 18 + 6 * matrix]
            for s, source in ((0, own), (1, core)):
                copies.append(pltpu.make_async_copy(source, target.at[s], sems.at[len(copies)]))
            for i, source in enumerate(halves):
                size = source.shape[0]
                start = pl.multiple_of((at[4] ^ (i % 2)) * size, size)
                copies.append(
                    pltpu.make_async_copy(source, target.at[2 + i // 2, pl.ds(start, size), :], sems.at[len(copies)])
                )
        for copy in copies:
            copy.start()
        needed = ((0,), (1,), (2, 3), (4, 5))
        biases = (
            b1[...],
            from_terms(close_terms[...][0:3]),
            from_terms(far_terms[...][0:3]),
            from_terms(far_terms[...][3:6]),
        )
        trio, mixed, dsecond_low, sums = outs
        second = after[...] + (kept[...] + close[...].astype(F32) + distant[...].astype(F32)) + out_bias[...]
        normed_mid, inverse_mid = norm_stats(second)
        mid = normed_mid * gain[1:2] + shift[1:2]
        mid_low = mid.astype(BF)
        trio[0] = mid_low
        total = jnp.zeros((rows, width), F32)
        for s in range(4):
            for i in needed[s]:
                copies[i].wait()
            pre = mm(mid_low, f1[s]) + biases[s]
            hidden, slope[s] = gelu_pair(pre)
            for i in needed[s]:
                copies[6 + i].wait()
            total = total + mm(hidden, f2[s])
        last = mid + total + fc2_bias[...]
        normed_last, inverse_last = norm_stats(last)
        first_row = (2 * at[0] + at[1]) * rows
        live = (first_row + lax.broadcasted_iota(jnp.int32, (rows, 1), 0) < at[3]).astype(F32)
        mixed[...] = ((normed_last * gain[2:3] + shift[2:3]) * live).astype(BF)
        delta = cot[...].astype(F32) * live
        dlast = norm_backward(delta, normed_last, inverse_last, gain[2:3])
        dlast_low = dlast.astype(BF)
        trio[1] = dlast_low
        dmid = dlast
        for s in range(4):
            dpre = (mm(dlast_low, f2[s], NT) * slope[s]).astype(BF)
            dmid = dmid + mm(dpre, f1[s], NT)
        dsecond = norm_backward(dmid, normed_mid, inverse_mid, gain[1:2])
        dsecond_low[...] = dsecond.astype(BF)
        sums[...] = jnp.concatenate(
            [
                column_sum(delta * normed_last),
                column_sum(delta),
                column_sum(dlast),
                column_sum(dmid * normed_mid),
                column_sum(dmid),
                column_sum(dsecond),
                jnp.zeros((2, width), F32),
            ],
            axis=0,
        )

    quarter = lambda ref, at: ref.at[rows_at(at[1], rows), :]
    tail = lambda ref, at: ref.at[pl.ds(base, 16), :]
    return launch(
        body,
        "feed",
        at,
        [
            near(after, quarter),
            near(kept, quarter),
            near(close, quarter),
            near(distant),
            near(cot, lambda ref, at: ref.at[rows_at(2 * at[0] + at[1], rows), :]),
            near(out_bias),
            near(fc2_bias),
            near(gain),
            near(shift),
            near(b1),
            near(terms[0], tail),
            near(terms[1], tail),
        ]
        + [raw(a) for group in weights for a in group],
        [shape(2, rows, width, dtype=BF), shape(rows, width, dtype=BF), shape(rows, width, dtype=BF), shape(8, width)],
        scratch=[
            pltpu.VMEM((4, width, units), BF),
            pltpu.VMEM((4, units, width), BF),
            pltpu.VMEM((4, rows, units), F32),
            pltpu.SemaphoreType.DMA((12,)),
        ],
        mib=20,
        us=10,
    )


def assemble(at, z, blocks):
    rows = blocks[0].shape[0]
    for base, own, distant in ((0, blocks[0], blocks[2]), (2 * rows, blocks[1], blocks[3])):
        z[pl.ds(pl.multiple_of(base + at[1] * rows, rows), rows), :] = own[...]
        z[pl.ds(pl.multiple_of(base + (1 - at[1]) * rows, rows), rows), :] = distant[...]


def cross_backward(at, z_blocks, raised, inverse, query, keys, values, w, wo, nh):
    rows, width = z_blocks[0].shape
    rows = 4 * rows
    half = rows // 2
    local = w.shape[1]
    hd = local // nh
    slots = keys.shape[1]
    scale = hd**-0.5

    def body(at, ins, outs, scratch):
        blocks, (wo, inverse, values, raised, query, keys, w) = ins[:4], ins[4:]
        keep, send, dquery, dkv, sums = outs
        z, douts, right, found = scratch
        assemble(at, z, blocks)
        zero = jnp.zeros((half, hd), BF)
        head_sum = jnp.zeros((1, local), F32)
        for r in range(2):
            span = slice(r * half, (r + 1) * half)
            dhead = mm(z[span, :], wo[...], NT)
            head_sum = head_sum + column_sum(dhead)
            scaled = query[span, :] * jnp.asarray(scale, BF)
            for h in range(nh):
                part = slice(h * hd, (h + 1) * hd)
                dout = (dhead[:, part] * inverse[h, span, 0:1]).astype(BF)
                douts[h, span, :] = jnp.concatenate([dout, dout], axis=1)
                right[h, 0, span, :] = jnp.concatenate([scaled[:, part], zero], axis=1)
                right[h, 1, span, :] = jnp.concatenate([zero, dout], axis=1)

        def one_head(h, _):
            grad = None
            for r in range(2):
                span = slice(r * half, (r + 1) * half)
                dprob = mm(douts[h, span, :], values[h], NT)
                low = raised[h, span, :]
                e = low.astype(F32)
                weighed = e * dprob
                mean = jnp.sum(weighed, axis=1, keepdims=True) * inverse[h, span, 0:1]
                dscore = (weighed - e * mean).astype(BF)
                both = mm(dscore, keys[h])
                found[h, span, :] = both[:, :hd] + both[:, hd:]
                part = mm(dscore, right[h, 0, span, :], TN) + mm(low, right[h, 1, span, :], TN)
                grad = part if grad is None else grad + part
            dkv[h] = grad.astype(BF)
            return 0

        lax.fori_loop(0, nh, one_head, 0)
        query_sum = jnp.zeros((1, local), F32)
        for r, target in enumerate((keep, send)):
            span = slice(r * half, (r + 1) * half)
            dq = jnp.concatenate([found[h, span, :] for h in range(nh)], axis=1) * scale
            query_sum = query_sum + column_sum(dq)
            dq_low = dq.astype(BF)
            dquery[span, :] = dq_low
            target[...] = mm(dq_low, w[0]).astype(target.dtype)
        sums[...] = jnp.concatenate([query_sum, head_sum], axis=0)

    return launch(
        body,
        "cross_bwd",
        at,
        [near(a) for a in (*z_blocks, wo, inverse, values, raised, query, keys, w)],
        [
            shape(half, width),
            shape(half, width, dtype=BF),
            shape(rows, local, dtype=BF),
            shape(nh, slots, 2 * hd, dtype=BF),
            shape(2, local),
        ],
        scratch=[
            pltpu.VMEM((rows, width), BF),
            pltpu.VMEM((nh, rows, 2 * hd), BF),
            pltpu.VMEM((nh, 2, rows, 2 * hd), BF),
            pltpu.VMEM((nh, rows, hd), F32),
        ],
        mib=30,
        us=11,
    )


def store_gradient(at, dkv, w, nh):
    _, slots, twice = dkv.shape
    _, local, width = w.shape
    hd = twice // 2
    seg = slots // 4

    def body(at, ins, outs, _):
        dkv, w = ins
        keep, send = outs
        weights = []
        for h in range(nh):
            part = slice(h * hd, (h + 1) * hd)
            weights += [w[1][part], w[2][part]]
        weight = jnp.concatenate(weights, axis=0)
        for slot in (1, 3, 0, 2):
            rows = jnp.concatenate([dkv[h, slot * seg : (slot + 1) * seg, :] for h in range(nh)], axis=1)
            part = mm(rows, weight)
            if slot % 2 == 0:
                keep[slot // 2] = part
            else:
                send[slot // 2] = part.astype(BF)

    return launch(
        body,
        "store_grad",
        at,
        [near(dkv), near(w)],
        [shape(2, seg, width), shape(2, seg, width, dtype=BF)],
        us=2.6,
    )


def group_outs(width, columns, blocks, extra):
    if not blocks:
        return [shape(width, columns)]
    n, r = blocks
    tail = 3 * EXTRA if extra else 0
    return [shape(n * r + tail, columns, dtype=BF), shape(n, r, columns)]


def emit_group(at, grad, outs, blocks, first, columns, late=False):
    if not blocks:
        outs[0][:, first : first + columns] = grad[...]
        return
    n, r = blocks
    span = slice(first, first + columns)
    for b in range(n):
        mine = 4 * (b % 2) + 2 * at[5] + b // 2 if late else 2 * b + at[4]
        theirs = 4 * (b % 2) + 2 * (1 - at[5]) + b // 2 if late else 2 * b + 1 - at[4]
        outs[0][b * r : (b + 1) * r, span] = grad[pl.ds(pl.multiple_of(theirs * r, 8), r), :].astype(BF)
        outs[1][b, :, span] = grad[pl.ds(pl.multiple_of(mine * r, 8), r), :]


def turned_product(out, left, right, step=256):
    if left.shape[1] % step:
        out[...] = mm(left[...], right[...], TN)
        return

    def some(i, _):
        span = pl.ds(pl.multiple_of(i * step, step), step)
        out[span, :] = mm(left[:, span], right[...], TN)
        return 0

    lax.fori_loop(0, left.shape[1] // step, some, 0)


def feed_grads(at, trios, fc1, fc2, b1, blocks):
    _, rows, width = trios[0].shape
    units = fc1.shape[1]

    def body(at, ins, outs, scratch):
        trios, (f1, f2, b1) = ins[:4], ins[4:]
        mid, dlast, hidden, dpre, grad = scratch
        for s, block in enumerate(trios):
            mid[s * rows : (s + 1) * rows, :] = block[0]
            dlast[s * rows : (s + 1) * rows, :] = block[1]

        f1.ready()
        f2.ready()

        def some_rows(i, total):
            span = rows_at(i, 2 * rows)
            hidden[span, :], slope = gelu_pair(mm(mid[span, :], f1[...]) + b1[...])
            grad_pre = mm(dlast[span, :], f2[...], NT) * slope
            dpre[span, :] = grad_pre.astype(BF)
            return total + column_sum(grad_pre)

        outs[-1][...] = lax.fori_loop(0, 2, some_rows, jnp.zeros((1, units), F32))
        turned_product(grad, mid, dpre)
        emit_group(at, grad, outs, blocks, 0, units, True)
        turned_product(grad, dlast, hidden)
        emit_group(at, grad, outs, blocks, units, units, True)

    return launch(
        body,
        "feed_grads",
        at,
        [near(a) for a in trios] + [far(fc1), far(fc2), near(b1)],
        group_outs(width, 2 * units, blocks, False) + [shape(1, units)],
        scratch=[pltpu.VMEM((4 * rows, width), BF)] * 2
        + [pltpu.VMEM((4 * rows, units), BF)] * 2
        + [pltpu.VMEM((width, units), F32)],
        mib=20,
        us=6,
    )


def cross_grads(at, z_blocks, mine, other, dquery, heads, shards, dkv, first_mine, first_other, flat, small, nh, blocks):
    half, width = mine.shape
    local = dquery.shape[1]
    hd = local // nh
    seg = shards[0].shape[0]
    feed_sums, first_sums, fc1_sum, head_sums = small

    def body(at, ins, outs, scratch):
        z_blocks, shards = ins[0:4], ins[4:8]
        mine, other, dquery, heads, dkv, first_mine, first_other, flat, feed_sums, first_sums, fc1_sum, head_sums = ins[8:]
        z, grad = scratch
        extra = outs[-1]
        assemble(at, z, z_blocks)
        grad[...] = mm(mine[...], dquery[:half], TN) + mm(other[...], dquery[half:], TN)
        emit_group(at, grad, outs, blocks, 0, local)
        grad[...] = mm(z[...], heads[...], TN)
        emit_group(at, grad, outs, blocks, 3 * local, local)
        z[rows_at(at[0], half), :] = first_mine[...]
        z[rows_at(1 - at[0], half), :] = first_other[...]
        grad[...] = mm(z[...], flat[...], TN)
        emit_group(at, grad, outs, blocks, 4 * local, local)
        both = None
        for slot, block in enumerate(shards):
            rows = jnp.concatenate([dkv[h, slot * seg : (slot + 1) * seg, :] for h in range(nh)], axis=1)
            part = mm(block[...], rows, TN)
            both = part if both is None else both + part
        for i in range(2):
            grad[...] = jnp.concatenate([both[:, (2 * h + i) * hd : (2 * h + i + 1) * hd] for h in range(nh)], axis=1)
            emit_group(at, grad, outs, blocks, (1 + i) * local, local)
        line = jnp.concatenate([head_sums[0:1], head_sums[1:2], jnp.zeros((1, width - 2 * local), F32)], axis=1)
        small = jnp.concatenate(
            [feed_sums[0:6], first_sums[0:3], fc1_sum[...], line, jnp.zeros((EXTRA - 11, width), F32)], axis=0
        )
        extra[...] = small
        if blocks:
            outs[0][blocks[0] * blocks[1] :, 0:width] = three_terms(small)
            outs[0][blocks[0] * blocks[1] :, width:] = jnp.zeros((3 * EXTRA, 5 * local - width), BF)

    return launch(
        body,
        "cross_grads",
        at,
        [
            near(a)
            for a in (
                *z_blocks,
                *shards,
                mine,
                other,
                dquery,
                heads,
                dkv,
                first_mine,
                first_other,
                flat,
                feed_sums,
                first_sums,
                fc1_sum,
                head_sums,
            )
        ],
        group_outs(width, 5 * local, blocks, True) + [shape(EXTRA, width)],
        scratch=[pltpu.VMEM((2 * half, width), BF), pltpu.VMEM((width, local), F32)],
        us=4,
    )


def first_back(at, z_own, z_distant, mine, other, total, gain):
    half, width = mine.shape
    rows = half // 2

    def body(at, ins, outs, scratch):
        z_own, z_distant, mine, other, total, gain = ins
        dfirst, low, sums = outs
        (dafter,) = scratch
        dafter[rows_at(at[1], rows), :] = z_own[...].astype(F32)
        dafter[rows_at(1 - at[1], rows), :] = z_distant[...].astype(F32)
        value = dafter[...] + (mine[...].astype(F32) + other[...].astype(F32))
        normed, inverse = norm_stats(total[...])
        result = norm_backward(value, normed, inverse, gain[0:1])
        dfirst[...] = result
        low[...] = result.astype(BF)
        place = lax.broadcasted_iota(jnp.int32, (half, 1), 0)
        counted = ((place >= at[1] * rows) & (place < (at[1] + 1) * rows)).astype(F32)
        sums[...] = jnp.concatenate(
            [
                column_sum(value * normed * counted),
                column_sum(value * counted),
                column_sum(result * counted),
                jnp.zeros((5, width), F32),
            ],
            axis=0,
        )

    return launch(
        body,
        "first_back",
        at,
        [near(a) for a in (z_own, z_distant, mine, other, total, gain)],
        [shape(half, width), shape(half, width, dtype=BF), shape(8, width)],
        scratch=[pltpu.VMEM((half, width), F32)],
        us=2.8,
    )


def self_backward(at, mine, other, tokens, w, wo, qkv, prob, mixed, nh, blocks):
    half, width = mine.shape
    rows = 2 * half
    local = wo.shape[0]
    hd = local // nh
    scale = hd**-0.5

    def body(at, ins, outs, scratch):
        mine, other, wo, qkv, prob, tok, w, mixed = ins
        send, keep = outs[0:2]
        group, extra = outs[2:-1], outs[-1]
        z, dqkv, grad = scratch
        own, distant = rows_at(at[0], half), rows_at(1 - at[0], half)
        z[own, :] = mine[...]
        z[distant, :] = other[...]
        dself = mm(z[...], wo[...], NT).astype(BF)
        v, k, q = qkv[2], qkv[1], qkv[0]
        dq, dk, dv = [], [], []
        for h in range(nh):
            part = slice(h * hd, (h + 1) * hd)
            weights_low = prob[h]
            weights = weights_low.astype(F32)
            weighed = weights * mm(dself[:, part], v[:, part], NT)
            dscore = (weighed - weights * jnp.sum(weighed, axis=1, keepdims=True)).astype(BF)
            dq.append(mm(dscore, k[:, part]))
            dk.append(mm(dscore, q[:, part], TN))
            dv.append(mm(weights_low, dself[:, part], TN))
        dquery = jnp.concatenate(dq, axis=1) * scale
        dvalue = jnp.concatenate(dv, axis=1)
        dqkv[0] = dquery.astype(BF)
        dqkv[1] = (jnp.concatenate(dk, axis=1) * scale).astype(BF)
        dqkv[2] = dvalue.astype(BF)
        x = tok[...]
        for i in range(3):
            grad[...] = mm(x, dqkv[i], TN)
            emit_group(at, grad, group, blocks, i * local, local)
        line = jnp.concatenate([column_sum(dquery), column_sum(dvalue), jnp.zeros((1, local), F32)], axis=1)
        small = jnp.concatenate([line, jnp.zeros((EXTRA - 1, 3 * local), F32)], axis=0)
        extra[...] = small
        if blocks:
            group[0][blocks[0] * blocks[1] :, :] = three_terms(small)
        send[half:, :] = mixed[...]
        for place, out in ((distant, send), (own, keep)):
            total = mm(dqkv[0, place, :], w[0]) + mm(dqkv[1, place, :], w[1]) + mm(dqkv[2, place, :], w[2])
            out[0:half, :] = total.astype(out.dtype)

    return launch(
        body,
        "self_bwd",
        at,
        [near(a) for a in (mine, other, wo, qkv, prob, tokens, w, mixed)],
        [shape(half + half // 2, width, dtype=BF), shape(half, width)]
        + group_outs(width, 3 * local, blocks, True)
        + [shape(EXTRA, 3 * local)],
        scratch=[
            pltpu.VMEM((rows, width), BF),
            pltpu.VMEM((3, rows, local), BF),
            pltpu.VMEM((width, local), F32),
        ],
        mib=20,
        us=6,
    )


def add_stage(at, keep, got, small, bit):
    n, rows, columns = keep.shape
    tail = 0 if small is None else 3 * EXTRA
    reach = small.shape[1] if tail else 0

    def body(at, ins, outs, _):
        keep, got = ins[:2]
        mine = at[bit]
        send, stay = outs[:2]
        for b in range(n // 2):
            for chosen, out in ((1 - mine, send), (mine, stay)):
                block = 2 * b + chosen
                value = keep[block] + got[pl.ds(pl.multiple_of(block * rows, 8), rows), :].astype(F32)
                if out is send:
                    send[b * rows : (b + 1) * rows, :] = value.astype(BF)
                else:
                    stay[b] = value
        if tail:
            total = ins[2][...] + from_terms(got[n * rows :, 0:reach])
            outs[2][...] = total
            send[n // 2 * rows :, 0:reach] = three_terms(total)
            if reach < columns:
                send[n // 2 * rows :, reach:] = jnp.zeros((tail, columns - reach), BF)

    ins = [near(keep), near(got)] + ([near(small)] if tail else [])
    outs = [shape(n // 2 * rows + tail, columns, dtype=BF), shape(n // 2, rows, columns)]
    if tail:
        outs.append(shape(EXTRA, reach))
    return launch(body, "add_stage", at, ins, outs, us=1)


def last_stage(at, keep, got, small, parts):
    _, rows, columns = keep.shape
    each = columns // sum(count for count, _ in parts)
    reach = 0 if small is None else small.shape[1]

    def body(at, ins, outs, _):
        total = ins[0][0] + ins[1][0:rows].astype(F32)
        first = 0
        for out, (count, turned) in zip(outs, parts):
            if count == 1:
                value = total[:, first * each : (first + 1) * each]
                out[...] = value.T if turned else value
            else:
                for i in range(count):
                    out[i] = total[:, (first + i) * each : (first + i + 1) * each]
            first += count
        if reach:
            outs[-1][...] = ins[2][...] + from_terms(ins[1][rows:, 0:reach])

    outs = []
    for count, turned in parts:
        dims = (rows, each) if count == 1 else (count, rows, each)
        outs.append(shape(*(dims[::-1] if turned else dims)))
    ins = [near(keep), near(got)]
    if reach:
        ins.append(near(small))
        outs.append(shape(EXTRA, reach))
    return launch(body, "last_stage", at, ins, outs, us=1)


def join_halves(at, mine, other):
    half, width = mine.shape

    def body(at, ins, outs, _):
        outs[0][rows_at(at[0], half), :] = ins[0][...]
        outs[0][rows_at(1 - at[0], half), :] = ins[1][...]

    out = shape(2 * half, width, dtype=mine.dtype)
    return launch(body, "join_halves", at, [near(mine), near(other)], [out])[0]


def join_quarters(at, own, close, distant):
    rows, width = own.shape

    def body(at, ins, outs, _):
        for flips, block in enumerate(ins):
            place = 2 * (at[0] ^ (flips & 1)) + (at[1] ^ (flips >> 1))
            outs[0][rows_at(place, rows), :] = block[...]

    part = lambda i: lambda ref, at: ref.at[pl.ds(i * rows, rows), :]
    ins = [near(own), near(close, part(2)), near(distant, part(2)), near(distant, part(3))]
    return launch(body, "join_quarters", at, ins, [shape(4 * rows, width, dtype=BF)])[0]


def flip(bit, size):
    return [(i, i ^ bit) for i in range(size)]


def butterfly(value, axis, size):
    bit = 1
    while bit < size:
        value = value + lax.ppermute(value, axis, flip(bit, size))
        bit *= 2
    return value


def on_device(
    tokens,
    store,
    summary_length,
    top_index,
    cotangent,
    self_qkv_weight,
    self_qv_bias,
    self_out_weight,
    self_out_bias,
    qkv_weight,
    qv_bias,
    out_weight,
    out_bias,
    fc1_weight,
    fc1_bias,
    fc2_weight,
    fc2_bias,
    norm_gain,
    norm_shift,
):
    rows, width = tokens.shape
    half, quarter = rows // 2, rows // 4
    nh = top_index.shape[1]
    local = qkv_weight.shape[2]
    units = fc1_weight.shape[1]
    seg = store.shape[1]
    wide = lax.axis_size("wide")
    place = lax.axis_index("narrow")
    doc = lax.axis_index("wide")
    core, across = place % 2, place // 2
    at = jnp.stack([core, across, place, summary_length[0], doc % 2, doc // 2 % 2, doc // 4]).astype(jnp.int32)
    blocks = (wide // 2, width // wide) if wide == 8 else None
    row = lambda v: v.reshape(1, -1)
    self_w = jnp.swapaxes(self_qkv_weight, 1, 2)
    cross_w = jnp.swapaxes(qkv_weight, 1, 2)

    def to_core(v):
        return lax.ppermute(v, "narrow", CORE)

    def to_across(v):
        return lax.ppermute(v, "narrow", ACROSS)

    def spread(v):
        distant = to_across(v)
        return [v, to_core(v), distant, to_core(distant)]

    def chip_sum(keep, send):
        return (keep + to_core(send).astype(F32)).astype(BF)

    store_x = to_across(store[0])
    qkv, prob, flat, send, keep = self_forward(
        at, tokens, self_w, self_qv_bias, self_out_weight, row(fc1_bias), nh
    )
    close = to_core(send)
    mine = jnp.concatenate(
        [
            (keep + close[:half].astype(F32)).astype(BF),
            send[half : half + 3],
            close[half : half + 3],
            jnp.zeros((16 - 6, width), BF),
        ],
        axis=0,
    )
    terms_close = close
    other = to_across(mine)
    doc_bit = doc % 2
    share = lambda v: lax.dynamic_slice_in_dim(v, doc_bit * (v.shape[0] // 2), v.shape[0] // 2, 0)
    over = lambda v, bit: lax.ppermute(v, "wide", flip(bit, wide))
    f1_half, f2_half = tie((share(fc1_weight), share(fc2_weight)), mine)
    f1_x, f2_x = to_across(f1_half), to_across(f2_half)
    index = index_rows(top_index)
    bias_mine = make_mask(tie(at, mine, f1_half, f2_half), index, top_index.shape, seg, 128, 0)
    store_x = tie(store_x, bias_mine)
    shards = [store[0], to_core(tie(store[0], bias_mine)), store_x, to_core(store_x)]
    bias_other = make_mask(tie(at, bias_mine), index, top_index.shape, seg, 128, 1)
    other, f1_x = tie((other, f1_x), bias_other)
    f1_y = over(f1_x, 1)
    first_total, after, after_low = first_norm(at, mine, other, tokens, row(self_out_bias), norm_gain, norm_shift)
    after_other = to_core(after_low)

    keys, values = keys_values(tie(at, after_low), shards, cross_w, nh)
    f1_core = to_core(tie(fc1_weight, keys))
    keep, send, raised, inverse, query, heads = cross_forward(
        tie(at, keys), after_low, after_other, bias_mine, bias_other, keys, values, cross_w, qv_bias, out_weight, nh
    )
    close = to_core(send)
    theirs = (1 - across) * quarter
    distant = to_across(
        (
            lax.dynamic_slice_in_dim(keep, theirs, quarter, 0)
            + lax.dynamic_slice_in_dim(close, theirs, quarter, 0).astype(F32)
        ).astype(BF)
    )
    f2_x = tie(f2_x, keep)
    f2_y = over(f2_x, 1)
    f2_core = to_core(tie(fc2_weight, keep))
    f1_y = tie(f1_y, close)
    f2_y = tie(f2_y, distant)
    weights = (
        (fc1_weight, f1_core, f1_x, f1_y, to_core(f1_x), to_core(f1_y)),
        (fc2_weight, f2_core, f2_x, f2_y, to_core(f2_x), to_core(f2_y)),
    )

    pair, mixed_own, z, feed_sums = feed(
        at,
        after,
        keep,
        close,
        distant,
        cotangent,
        weights,
        row(fc1_bias),
        (terms_close, other),
        row(out_bias),
        row(fc2_bias),
        norm_gain,
        norm_shift,
    )
    z_all = spread(z)
    trios = spread(tie(pair, z_all[2]))

    keep, send, dquery, dkv, cross_sums = cross_backward(
        at, z_all, raised, inverse, query, keys, values, cross_w, out_weight, nh
    )
    mine = chip_sum(keep, send)
    other = to_across(mine)
    *feed_out, fc1_sum = feed_grads(tie(at, mine), trios, fc1_weight, fc2_weight, row(fc1_bias), blocks)
    other = tie(other, fc1_sum)
    dfirst, dfirst_low, first_sums = first_back(at, z_all[0], z_all[2], mine, other, first_total, norm_gain)
    dfirst_other = to_core(dfirst_low)
    store_keep, store_send = store_gradient(tie(at, dfirst_low), dkv, cross_w, nh)
    store_close = to_core(store_send)
    *cross_out, cross_small = cross_grads(
        tie(at, store_send),
        z_all,
        after_low,
        after_other,
        dquery,
        heads,
        shards,
        dkv,
        dfirst_low,
        dfirst_other,
        flat,
        (feed_sums, first_sums, fc1_sum, cross_sums),
        nh,
        blocks,
    )
    store_distant = to_across((store_keep[1] + tie(store_close, cross_small)[1].astype(F32)).astype(BF))

    send, keep, *self_out, self_small = self_backward(
        tie(at, cross_small), dfirst_low, dfirst_other, tokens, self_w, self_out_weight, qkv, prob, mixed_own, nh, blocks
    )
    close = to_core(send)
    mine = jnp.concatenate([(keep + close[:half].astype(F32)).astype(BF), send[half:], close[half:]], axis=0)
    other = to_across(mine)
    tokens_half = dfirst + (mine[:half].astype(F32) + other[:half].astype(F32))
    tokens_grad = join_halves(at, tokens_half, to_core(tokens_half))
    mixed = join_quarters(at, mixed_own, close, other)
    store_grad = (store_keep[0] + store_close[0].astype(F32) + store_distant.astype(F32))[None]

    if blocks:
        feed_send, feed_keep = add_stage(tie(at, self_small), feed_out[1], over(feed_out[0], 2), None, 6)
        cross_send, cross_keep, cross_small = add_stage(
            tie(at, feed_send), cross_out[1], over(cross_out[0], 1), cross_small, 5
        )
        self_send, self_keep, self_small = add_stage(
            tie(at, cross_send), self_out[1], over(self_out[0], 1), self_small, 5
        )
        feed_send, feed_keep = add_stage(tie(at, self_send), feed_keep, over(feed_send, 4), None, 4)
        cross_send, cross_keep, cross_small = add_stage(
            tie(at, feed_send), cross_keep, over(cross_send, 2), cross_small, 6
        )
        self_send, self_keep, self_small = add_stage(
            tie(at, cross_send), self_keep, over(self_send, 2), self_small, 6
        )
        fc1_grad, fc2_grad = last_stage(tie(at, self_send), feed_keep, over(feed_send, 1), None, [(1, False), (1, False)])
        fc2_grad = fc2_grad.T
        qkv_grad, out_grad, self_out_grad, cross_small = last_stage(
            tie(at, fc1_grad), cross_keep, over(cross_send, 4), cross_small, [(3, False), (1, True), (1, True)]
        )
        self_qkv_grad, self_small = last_stage(
            tie(at, cross_small), self_keep, over(self_send, 4), self_small, [(3, False)]
        )
    else:
        scatter = functools.partial(lax.psum_scatter, axis_name="wide", tiled=True)
        parts = lambda g: jnp.stack([g[:, i * local : (i + 1) * local] for i in range(3)])
        fc1_grad = scatter(feed_out[0][:, :units], scatter_dimension=0)
        fc2_grad = scatter(feed_out[0][:, units:].T, scatter_dimension=1)
        qkv_grad = scatter(parts(cross_out[0]), scatter_dimension=1)
        out_grad = scatter(cross_out[0][:, 3 * local : 4 * local].T, scatter_dimension=1)
        self_qkv_grad = scatter(parts(self_out[0]), scatter_dimension=1)
        self_out_grad = scatter(cross_out[0][:, 4 * local :].T, scatter_dimension=1)
        cross_small = butterfly(cross_small, "wide", wide)
        self_small = butterfly(self_small, "wide", wide)
    summed = butterfly(cross_small, "narrow", 4)
    gain_last, shift_last, fc2_b, gain_mid, shift_mid, out_b, gain_first, shift_first, self_out_b = (
        summed[i] for i in range(9)
    )
    return (
        mixed,
        tokens_grad,
        store_grad,
        self_qkv_grad,
        self_small[0, : 2 * local].reshape(2, local),
        self_out_grad,
        self_out_b,
        qkv_grad,
        cross_small[10, : 2 * local].reshape(2, local),
        out_grad,
        out_b,
        fc1_grad,
        cross_small[9],
        fc2_grad,
        fc2_b,
        jnp.stack([gain_first, gain_mid, gain_last]),
        jnp.stack([shift_first, shift_mid, shift_last]),
    )


def solution(mesh):
    placed = (
        P("wide", None),
        P("wide", "narrow", None),
        P("wide"),
        P("wide", "narrow", None, None),
        P("wide", None),
        P(None, None, "narrow"),
        P(None, "narrow"),
        P("narrow", None),
        P(),
        P(None, None, "narrow"),
        P(None, "narrow"),
        P("narrow", None),
        P(),
        P(None, "narrow"),
        P("narrow"),
        P("narrow", None),
        P(),
        P(),
        P(),
    )
    return jax.shard_map(
        on_device,
        mesh=mesh,
        in_specs=placed,
        out_specs=(
            P("wide", None),
            P("wide", None),
            P("wide", "narrow", None),
            P(None, "wide", "narrow"),
            P(None, "narrow"),
            P("narrow", "wide"),
            P(),
            P(None, "wide", "narrow"),
            P(None, "narrow"),
            P("narrow", "wide"),
            P(),
            P("wide", "narrow"),
            P("narrow"),
            P("narrow", "wide"),
            P(),
            P(),
            P(),
        ),
        check_vma=False,
    )
```

profile of v0, /device:TPU:0, one launch (start us, length us, event | category | flops | bytes accessed | tf_op | source)
XLA Modules:
  0.0 244.0 jit_solution(14594849562027535988)
XLA Ops:
  1.5 1.3 reshape.56.refs_4_.refs_9_.refs_6_
  3.4 7.5 %self_fwd.1 = (bf16[3,512,192]{2,1,0:T(8,128)(2,1)}, bf16[3,512,512]{2,1,0:T(8,128)(2,1)}, bf16[512,192]{1,0:T(8,128)(2,1)}, bf16[272,768]{1,0:T(8,128)(2,1)}, f32[256,768]{1,0:T(8,128)}) custom-call(s32[7]{0:T(128)} %stack.33.at_ref, bf16[512,768]{1,0:T(8,128)(2,1)} %refs_5_.7, bf16[3,192,768]{2,1,0:T(8,128)(2,1)} %bitcast.31, bf16[192,768]{1,0:T(8,128)(2,1)} %refs_2_.5, ...), custom_call_target="tpu_custom_call" | custom-call | flops 440000000 | bytes 1000 | tf_op jit(solution)/shard_map/self_fwd/pallas_call | solution.py:160
  11.4 2.6 %collective-permute-start.4 = (bf16[416,768]{1,0:T(8,128)(2,1)S(1)}, bf16[416,768]{1,0:T(8,128)(2,1)S(1)}, u32[]{:S(2)}, u32[]{:S(2)}) collective-permute-start(bf16[416,768]{1,0:T(8,128)(2,1)S(1)} %bitcast.33), channel_id=1, source_target_pairs={{0,2},{1,3},{2,0},{3,1},{4,6},{5,7},{6,4},{7,5},{8,10},{9,11},{10,... | collective-permute-start | bytes 1916936 | tf_op jit(solution)/shard_map/ppermute | solution.py:1094
  14.7 1.2 constant_dynamic-slice_fusion
  16.3 2.0 collective-permute-start.1
  18.4 2.8 %copy-done = s32[512,3,4,256]{3,2,1,0:T(4,128)S(1)} copy-done((s32[512,3,4,256]{3,2,1,0:T(4,128)S(1)}, s32[512,3,4,256]{3,2,1,0:T(4,128)}, u32[]{:S(2)}) %copy-start) | copy-done | bytes 6291480
  21.1 9.8 %mask.2.refs_4_ = bf16[3,256,1664]{2,1,0:T(8,128)(2,1)S(1)} custom-call(s32[7]{0:T(128)S(1)} %copy-done.42, s32[4,3072,128]{2,1,0:T(8,128)S(1)} %bitcast.23), custom_call_target="tpu_custom_call" | custom-call | flops 1100000000 | bytes 1000 | tf_op jit(solution)/shard_map/mask/pallas_call | solution.py:160
  31.6 9.6 %mask.3.refs_5_ = bf16[3,256,1664]{2,1,0:T(8,128)(2,1)S(1)} custom-call(s32[7]{0:T(128)S(1)} %copy-done.42, s32[4,3072,128]{2,1,0:T(8,128)S(1)} %bitcast.24), custom_call_target="tpu_custom_call" | custom-call | flops 1100000000 | bytes 1000 | tf_op jit(solution)/shard_map/mask/pallas_call | solution.py:160
  41.2 9.3 %collective-permute-done.1.refs_1_.refs_11_ = bf16[272,768]{1,0:T(8,128)(2,1)S(1)} collective-permute-done((bf16[272,768]{1,0:T(8,128)(2,1)S(1)}, bf16[272,768]{1,0:T(8,128)(2,1)S(1)}, u32[]{:S(2)}, u32[]{:S(2)}) %collective-permute-start.1) | collective-permute-done | bytes 417824 | tf_op jit(solution)/shard_map/ppermute | solution.py:1094
  51.6 1.8 collective-permute-start.14
  53.5 2.2 keys_values.1
  55.9 7.5 %cross_fwd.1 = (f32[256,768]{1,0:T(8,128)S(1)}, bf16[256,768]{1,0:T(8,128)(2,1)S(1)}, bf16[3,512,1664]{2,1,0:T(8,128)(2,1)S(1)}, f32[3,512,128]{2,1,0:T(8,128)S(...) custom-call(s32[7]{0:T(128)S(1)} %copy-done.42, bf16[256,768]{1,0:T(8,128)(2,1)S(1)} %get-tuple-element.121.refs_0_.refs_8_, ...), custom_call_target="tpu_custom_call" | custom-call | flops 990000000 | bytes 1000 | tf_op jit(solution)/shard_map/cross_fwd/pallas_call | solution.py:160
  63.5 2.3 copy-done.6
  68.2 1.5 collective-permute-start.10
  70.8 1.2 add_convert_fusion.4
  72.0 12.6 %collective-permute-done.10.refs_15_ = bf16[384,768]{1,0:T(8,128)(2,1)} collective-permute-done((bf16[384,768]{1,0:T(8,128)(2,1)}, bf16[384,768]{1,0:T(8,128)(2,1)}, u32[]{:S(2)}, u32[]{:S(2)}) %collective-permute-start.10) | collective-permute-done | bytes 589856 | tf_op jit(solution)/shard_map/ppermute | solution.py:1121
  84.9 11.8 %collective-permute-done.15.refs_21_ = bf16[384,768]{1,0:T(8,128)(2,1)} collective-permute-done((bf16[384,768]{1,0:T(8,128)(2,1)}, bf16[384,768]{1,0:T(8,128)(2,1)}, u32[]{:S(2)}, u32[]{:S(2)}) %collective-permute-start.15) | collective-permute-done | bytes 589856 | tf_op jit(solution)/shard_map/ppermute | solution.py:1121
  97.3 1.6 collective-permute-done.16.refs_22_
  100.6 1.1 copy-done.23
  101.8 1.2 copy-done.25
  103.0 1.1 copy-done.37
  105.3 10.1 %feed.1 = (bf16[2,128,768]{2,1,0:T(8,128)(2,1)S(1)}, bf16[128,768]{1,0:T(8,128)(2,1)S(1)}, bf16[128,768]{1,0:T(8,128)(2,1)S(1)}, f32[8,768]{1,0:T(8,128)S(1)}) custom-call(s32[7]{0:T(128)S(1)} %copy-done.42, f32[256,768]{1,0:T(8,128)S(1)} %copy-done.41, f32[256,768]{1,0:T(8,128)S(1)} %copy-done.21, bf16[256,768]{1,0:T(8,128)(2,1)} %collective-permute-done.7.refs_2_, ...), custom_call_target="tpu_custom_call" | custom-call | flops 1100000000 | bytes 1000 | tf_op jit(solution)/shard_map/feed/pallas_call | solution.py:160
  115.8 6.6 %collective-permute-done.18.refs_2_.refs_1_ = bf16[128,768]{1,0:T(8,128)(2,1)S(1)} collective-permute-done((bf16[128,768]{1,0:T(8,128)(2,1)S(1)}, bf16[128,768]{1,0:T(8,128)(2,1)S(1)}, u32[]{:S(2)}, u32[]{:S(2)}) %collective-permute-start.18) | collective-permute-done | bytes 196640 | tf_op jit(solution)/shard_map/ppermute | solution.py:1094
  123.9 10.3 %cross_bwd.1 = (f32[256,768]{1,0:T(8,128)S(1)}, bf16[256,768]{1,0:T(8,128)(2,1)S(1)}, bf16[512,192]{1,0:T(8,128)(2,1)S(1)}, bf16[3,1664,128]{2,1,0:T(8,128)(2,1)S(1)}, f32[2,192]{1,0:T(2,128)S(1)}) custom-call(s32[7]{0:T(128)S(1)} %copy-done.42, bf16[128,768]{1,0:T(8,128)(2,1)S(1)} %get-tuple-element.137.refs_0_, ...), custom_call_target="tpu_custom_call" | custom-call | flops 1210000000 | bytes 1000 | tf_op jit(solution)/shard_map/cross_bwd/pallas_call | solution.py:160
  137.1 7.0 %feed_grads.1 = (bf16[384,1536]{1,0:T(8,128)(2,1)S(1)}, f32[4,96,1536]{2,1,0:T(8,128)S(1)}, f32[1,768]{1,0:T(1,128)S(1)}) custom-call(s32[7]{0:T(128)S(1)} %copy-done.42, bf16[2,128,768]{2,1,0:T(8,128)(2,1)S(1)} %get-tuple-element.145.refs_0_, bf16[2,128,768]{2,1,0:T(8,128)(2,1)S(1)} %collective-permute-done.23.refs_1_, ...), custom_call_target="tpu_custom_call" | custom-call | flops 660000000 | bytes 1000 | tf_op jit(solution)/shard_map/feed_grads/pallas_call | solution.py:160
  144.2 3.2 %collective-permute-done.22.refs_3_ = bf16[256,768]{1,0:T(8,128)(2,1)S(1)} collective-permute-done((bf16[256,768]{1,0:T(8,128)(2,1)S(1)}, bf16[256,768]{1,0:T(8,128)(2,1)S(1)}, u32[]{:S(2)}, u32[]{:S(2)}) %collective-permute-start.22) | collective-permute-done | bytes 393248 | tf_op jit(solution)/shard_map/ppermute | solution.py:1094
  147.4 1.4 first_back.1
  148.9 2.1 store_grad.1
  151.5 1.6 collective-permute-start.32
  153.2 3.9 %cross_grads.1 = (bf16[432,960]{1,0:T(8,128)(2,1)S(1)}, f32[4,96,960]{2,1,0:T(8,128)S(1)}, f32[16,768]{1,0:T(8,128)S(1)}) custom-call(s32[7]{0:T(128)S(1)} %copy-done.42, bf16[128,768]{1,0:T(8,128)(2,1)S(1)} %get-tuple-element.137.refs_0_, bf16[128,768]{1,0:T(8,128)(2,1)S(1)} %collective-permute-done.19.refs_1_, ...), custom_call_target="tpu_custom_call" | custom-call | flops 440000000 | bytes 1000 | tf_op jit(solution)/shard_map/cross_grads/pallas_call | solution.py:160
  157.1 5.1 %self_bwd.1 = (bf16[384,768]{1,0:T(8,128)(2,1)S(1)}, f32[256,768]{1,0:T(8,128)S(1)}, bf16[432,576]{1,0:T(8,128)(2,1)S(1)}, f32[4,96,576]{2,1,0:T(8,128)S(1)}, f32[16,576]{1,0:T(8,128)S(1)}) custom-call(s32[7]{0:T(128)S(1)} %copy-done.42, bf16[256,768]{1,0:T(8,128)(2,1)S(1)} %get-tuple-element.149.refs_13_.refs_0_, ...), custom_call_target="tpu_custom_call" | custom-call | flops 660000000 | bytes 1000 | tf_op jit(solution)/shard_map/self_bwd/pallas_call | solution.py:160
  162.3 1.6 collective-permute-start.33
  165.5 14.0 %collective-permute-done.32.refs_1_ = bf16[384,1536]{1,0:T(8,128)(2,1)S(1)} collective-permute-done((bf16[384,1536]{1,0:T(8,128)(2,1)S(1)}, bf16[384,1536]{1,0:T(8,128)(2,1)S(1)}, u32[]{:S(2)}, u32[]{:S(2)}) %collective-permute-start.32) | collective-permute-done | bytes 1179680 | tf_op jit(solution)/shard_map/ppermute | solution.py:1121
  180.2 2.7 %collective-permute-start.35 = (bf16[192,1536]{1,0:T(8,128)(2,1)S(1)}, bf16[192,1536]{1,0:T(8,128)(2,1)S(1)}, u32[]{:S(2)}, u32[]{:S(2)}) collective-permute-start(bf16[192,1536]{1,0:T(8,128)(2,1)S(1)} %get-tuple-element.173), channel_id=1, source_target_pairs={{0,16},{4,20},{8,24},{12,28},{16,0},{20,4},{24,8},{28,12},{1,17},{... | collective-permute-start | bytes 1769480 | tf_op jit(solution)/shard_map/ppermute | solution.py:1121
  182.9 2.0 collective-permute-done.33.refs_1_
  187.1 9.2 %collective-permute-done.34.refs_1_ = bf16[432,576]{1,0:T(8,128)(2,1)S(1)} collective-permute-done((bf16[432,576]{1,0:T(8,128)(2,1)S(1)}, bf16[432,576]{1,0:T(8,128)(2,1)S(1)}, u32[]{:S(2)}, u32[]{:S(2)}) %collective-permute-start.34) | collective-permute-done | bytes 497696 | tf_op jit(solution)/shard_map/ppermute | solution.py:1121
  197.5 10.9 %collective-permute-done.35.refs_1_ = bf16[192,1536]{1,0:T(8,128)(2,1)S(1)} collective-permute-done((bf16[192,1536]{1,0:T(8,128)(2,1)S(1)}, bf16[192,1536]{1,0:T(8,128)(2,1)S(1)}, u32[]{:S(2)}, u32[]{:S(2)}) %collective-permute-start.35) | collective-permute-done | bytes 589856 | tf_op jit(solution)/shard_map/ppermute | solution.py:1121
  209.1 1.6 collective-permute-start.38
  211.3 1.7 collective-permute-start.39
  213.0 5.1 %collective-permute-done.37.refs_1_ = bf16[240,576]{1,0:T(8,128)(2,1)S(1)} collective-permute-done((bf16[240,576]{1,0:T(8,128)(2,1)S(1)}, bf16[240,576]{1,0:T(8,128)(2,1)S(1)}, u32[]{:S(2)}, u32[]{:S(2)}) %collective-permute-start.37) | collective-permute-done | bytes 276512 | tf_op jit(solution)/shard_map/ppermute | solution.py:1121
  219.1 1.5 join_quarters.1
  220.6 1.4 last_stage.3
  222.0 1.2 fusion
  223.2 8.9 %collective-permute-done.39.refs_1_ = bf16[144,960]{1,0:T(8,128)(2,1)S(1)} collective-permute-done((bf16[144,960]{1,0:T(8,128)(2,1)S(1)}, bf16[144,960]{1,0:T(8,128)(2,1)S(1)}, u32[]{:S(2)}, u32[]{:S(2)}) %collective-permute-start.39) | collective-permute-done | bytes 276512 | tf_op jit(solution)/shard_map/ppermute | solution.py:1121
  232.1 1.5 last_stage.4
  234.3 1.4 last_stage.5
  237.8 2.1 collective-permute-done.42
  241.8 1.8 join_halves.1
  (210 shorter events, 29.3 us)
Async XLA Ops:
  10.8 5.1 %collective-permute-start = (bf16[272,768]{1,0:T(8,128)(2,1)}, bf16[272,768]{1,0:T(8,128)(2,1)S(1)}, u32[]{:S(2)}, u32[]{:S(2)}) collective-permute-start(bf16[272,768]{1,0:T(8,128)(2,1)} %get-tuple-element.114), channel_id=1, source_target_pairs={{0,1},{1,0},{2,3},{3,2},{4,5},{5,4},{6,7},{7,6},{8,9},{9,8},{10,11... | collective-permute-start | bytes 1253384 | tf_op jit(solution)/shard_map/ppermute | solution.py:1091
  11.4 19.7 %collective-permute-start.4 = (bf16[416,768]{1,0:T(8,128)(2,1)S(1)}, bf16[416,768]{1,0:T(8,128)(2,1)S(1)}, u32[]{:S(2)}, u32[]{:S(2)}) collective-permute-start(bf16[416,768]{1,0:T(8,128)(2,1)S(1)} %bitcast.33), channel_id=1, source_target_pairs={{0,2},{1,3},{2,0},{3,1},{4,6},{5,7},{6,4},{7,5},{8,10},{9,11},{10,... | collective-permute-start | bytes 1916936 | tf_op jit(solution)/shard_map/ppermute | solution.py:1094
  16.3 34.2 %collective-permute-start.2 = (bf16[384,768]{1,0:T(8,128)(2,1)S(1)}, bf16[384,768]{1,0:T(8,128)(2,1)}, u32[]{:S(2)}, u32[]{:S(2)}) collective-permute-start(bf16[384,768]{1,0:T(8,128)(2,1)S(1)} %get-tuple-element.115), channel_id=1, source_target_pairs={{0,2},{1,3},{2,0},{3,1},{4,6},{5,7},{6,4},{7,5},{8,10},{9,11},{10,... | collective-permute-start | bytes 1769480 | tf_op jit(solution)/shard_map/ppermute | solution.py:1094
  16.3 34.1 %collective-permute-start.1 = (bf16[272,768]{1,0:T(8,128)(2,1)S(1)}, bf16[272,768]{1,0:T(8,128)(2,1)S(1)}, u32[]{:S(2)}, u32[]{:S(2)}) collective-permute-start(bf16[272,768]{1,0:T(8,128)(2,1)S(1)} %maximum_maximum_fusion.refs_0_), channel_id=1, source_target_pairs={{0,2},{1,3},{2,0},{3,1},{4,6},{5,7},{6,4},{7,5},{8,10},{9,11},{10,... | collective-permute-start | bytes 1253384 | tf_op jit(solution)/shard_map/ppermute | solution.py:1094
  31.0 22.5 %collective-permute-start.3 = (bf16[416,768]{1,0:T(8,128)(2,1)S(1)}, bf16[416,768]{1,0:T(8,128)(2,1)S(1)}, u32[]{:S(2)}, u32[]{:S(2)}) collective-permute-start(bf16[416,768]{1,0:T(8,128)(2,1)S(1)} %bitcast.34), channel_id=1, source_target_pairs={{0,1},{1,0},{2,3},{3,2},{4,5},{5,4},{6,7},{7,6},{8,9},{9,8},{10,11... | collective-permute-start | bytes 1916936 | tf_op jit(solution)/shard_map/ppermute | solution.py:1091
  31.1 22.4 %collective-permute-start.5 = (bf16[416,768]{1,0:T(8,128)(2,1)S(1)}, bf16[416,768]{1,0:T(8,128)(2,1)S(1)}, u32[]{:S(2)}, u32[]{:S(2)}) collective-permute-start(bf16[416,768]{1,0:T(8,128)(2,1)S(1)} %collective-permute-done.4.refs_2_.refs_6_), channel_id=1, source_target_pairs={{0,1},{1,0},{2,3},{3,2},{4,5},{5,4},{6,7},{7,6},{8,9},{9,8},{10,11... | collective-permute-start | bytes 1916936 | tf_op jit(solution)/shard_map/ppermute | solution.py:1091
  51.5 4.3 %collective-permute-start.6 = (bf16[256,768]{1,0:T(8,128)(2,1)S(1)}, bf16[256,768]{1,0:T(8,128)(2,1)S(1)}, u32[]{:S(2)}, u32[]{:S(2)}) collective-permute-start(bf16[256,768]{1,0:T(8,128)(2,1)S(1)} %get-tuple-element.121.refs_0_.refs_8_), channel_id=1, source_target_pairs={{0,1},{1,0},{2,3},{3,2},{4,5},{5,4},{6,7},{7,6},{8,9},{9,8},{10,11... | collective-permute-start | bytes 1179656 | tf_op jit(solution)/shard_map/ppermute | solution.py:1091
  51.6 18.1 %collective-permute-start.14 = (bf16[384,768]{1,0:T(8,128)(2,1)S(1)}, bf16[384,768]{1,0:T(8,128)(2,1)}, u32[]{:S(2)}, u32[]{:S(2)}) collective-permute-start(bf16[384,768]{1,0:T(8,128)(2,1)S(1)} %get-tuple-element.116), channel_id=1, source_target_pairs={{0,2},{1,3},{2,0},{3,1},{4,6},{5,7},{6,4},{7,5},{8,10},{9,11},{10,... | collective-permute-start | bytes 1769480 | tf_op jit(solution)/shard_map/ppermute | solution.py:1094
  55.9 41.4 %copy-start.54 = (f32[768]{0:T(1024)S(1)}, f32[768]{0:T(1024)}, u32[]{:S(2)}) copy-start(f32[768]{0:T(1024)} %param.31) | copy-start | bytes 9220
  55.9 41.4 %copy-start.55 = (f32[768]{0:T(1024)S(1)}, f32[768]{0:T(1024)}, u32[]{:S(2)}) copy-start(f32[768]{0:T(1024)} %param.35) | copy-start | bytes 9220
  55.9 44.7 %copy-start.49 = (f32[1,768]{1,0:T(1,128)S(1)}, f32[1,768]{1,0:T(1,128)}, u32[]{:S(2)}) copy-start(f32[1,768]{1,0:T(1,128)} %reshape.56.refs_4_.refs_9_.refs_6_) | copy-start | bytes 9220
  68.0 2.7 %collective-permute-start.7 = (bf16[256,768]{1,0:T(8,128)(2,1)S(1)}, bf16[256,768]{1,0:T(8,128)(2,1)}, u32[]{:S(2)}, u32[]{:S(2)}) collective-permute-start(bf16[256,768]{1,0:T(8,128)(2,1)S(1)} %get-tuple-element.129), channel_id=1, source_target_pairs={{0,1},{1,0},{2,3},{3,2},{4,5},{5,4},{6,7},{7,6},{8,9},{9,8},{10,11... | collective-permute-start | bytes 1179656 | tf_op jit(solution)/shard_map/ppermute | solution.py:1091
  68.2 16.5 %collective-permute-start.10 = (bf16[384,768]{1,0:T(8,128)(2,1)}, bf16[384,768]{1,0:T(8,128)(2,1)}, u32[]{:S(2)}, u32[]{:S(2)}) collective-permute-start(bf16[384,768]{1,0:T(8,128)(2,1)} %collective-permute-done.2.refs_14_), channel_id=1, source_target_pairs={{0,4},{4,0},{8,12},{12,8},{16,20},{20,16},{24,28},{28,24},{1,5},{5... | collective-permute-start | bytes 1769480 | tf_op jit(solution)/shard_map/ppermute | solution.py:1121
  69.7 27.0 %collective-permute-start.15 = (bf16[384,768]{1,0:T(8,128)(2,1)}, bf16[384,768]{1,0:T(8,128)(2,1)}, u32[]{:S(2)}, u32[]{:S(2)}) collective-permute-start(bf16[384,768]{1,0:T(8,128)(2,1)} %collective-permute-done.14.refs_20_), channel_id=1, source_target_pairs={{0,4},{4,0},{8,12},{12,8},{16,20},{20,16},{24,28},{28,24},{1,5},{5... | collective-permute-start | bytes 1769480 | tf_op jit(solution)/shard_map/ppermute | solution.py:1121
  70.2 27.0 %collective-permute-start.11 = (bf16[384,768]{1,0:T(8,128)(2,1)}, bf16[384,768]{1,0:T(8,128)(2,1)}, u32[]{:S(2)}, u32[]{:S(2)}) collective-permute-start(bf16[384,768]{1,0:T(8,128)(2,1)} %collective-permute-done.2.refs_14_), channel_id=1, source_target_pairs={{0,1},{1,0},{2,3},{3,2},{4,5},{5,4},{6,7},{7,6},{8,9},{9,8},{10,11... | collective-permute-start | bytes 1769480 | tf_op jit(solution)/shard_map/ppermute | solution.py:1091
  70.2 29.6 %collective-permute-start.9 = (bf16[768,768]{1,0:T(8,128)(2,1)S(1)}, bf16[768,768]{1,0:T(8,128)(2,1)}, u32[]{:S(2)}, u32[]{:S(2)}) collective-permute-start(bf16[768,768]{1,0:T(8,128)(2,1)S(1)} %copy-done.2), channel_id=1, source_target_pairs={{0,1},{1,0},{2,3},{3,2},{4,5},{5,4},{6,7},{7,6},{8,9},{9,8},{10,11... | collective-permute-start | bytes 3538952 | tf_op jit(solution)/shard_map/ppermute | solution.py:1091
  70.7 29.9 %collective-permute-start.13 = (bf16[768,768]{1,0:T(8,128)(2,1)S(1)}, bf16[768,768]{1,0:T(8,128)(2,1)}, u32[]{:S(2)}, u32[]{:S(2)}) collective-permute-start(bf16[768,768]{1,0:T(8,128)(2,1)S(1)} %copy-done.3), channel_id=1, source_target_pairs={{0,1},{1,0},{2,3},{3,2},{4,5},{5,4},{6,7},{7,6},{8,9},{9,8},{10,11... | collective-permute-start | bytes 3538952 | tf_op jit(solution)/shard_map/ppermute | solution.py:1091
  70.8 29.8 %copy-start.21 = (f32[256,768]{1,0:T(8,128)S(1)}, f32[256,768]{1,0:T(8,128)}, u32[]{:S(2)}) copy-start(f32[256,768]{1,0:T(8,128)} %copy-done.20) | copy-start | bytes 2359300
  84.6 12.1 %collective-permute-start.8 = (bf16[128,768]{1,0:T(8,128)(2,1)S(1)}, bf16[128,768]{1,0:T(8,128)(2,1)S(1)}, u32[]{:S(2)}, u32[]{:S(2)}) collective-permute-start(bf16[128,768]{1,0:T(8,128)(2,1)S(1)} %add_convert_fusion.4), channel_id=1, source_target_pairs={{0,2},{1,3},{2,0},{3,1},{4,6},{5,7},{6,4},{7,5},{8,10},{9,11},{10,... | collective-permute-start | bytes 589832 | tf_op jit(solution)/shard_map/ppermute | solution.py:1094
  96.7 2.2 collective-permute-start.16
  96.7 3.1 %collective-permute-start.12 = (bf16[384,768]{1,0:T(8,128)(2,1)}, bf16[384,768]{1,0:T(8,128)(2,1)S(1)}, u32[]{:S(2)}, u32[]{:S(2)}) collective-permute-start(bf16[384,768]{1,0:T(8,128)(2,1)} %collective-permute-done.10.refs_15_), channel_id=1, source_target_pairs={{0,1},{1,0},{2,3},{3,2},{4,5},{5,4},{6,7},{7,6},{8,9},{9,8},{10,11... | collective-permute-start | bytes 1769480 | tf_op jit(solution)/shard_map/ppermute | solution.py:1091
  97.2 3.4 %collective-permute-start.17 = (bf16[384,768]{1,0:T(8,128)(2,1)}, bf16[384,768]{1,0:T(8,128)(2,1)S(1)}, u32[]{:S(2)}, u32[]{:S(2)}) collective-permute-start(bf16[384,768]{1,0:T(8,128)(2,1)} %collective-permute-done.15.refs_21_), channel_id=1, source_target_pairs={{0,1},{1,0},{2,3},{3,2},{4,5},{5,4},{6,7},{7,6},{8,9},{9,8},{10,11... | collective-permute-start | bytes 1769480 | tf_op jit(solution)/shard_map/ppermute | solution.py:1091
  100.6 23.2 %slice-start = ((s8[5111808]{0:T(1024)(128)(4,1)}), s8[4194304]{0:T(1024)(128)(4,1)S(1)}, s32[]{:S(2)}) async-start(s8[5111808]{0:T(1024)(128)(4,1)} %bitcast.29), calls=%async_computation | async-start | bytes 8388608
  115.4 7.0 %collective-permute-start.18 = (bf16[128,768]{1,0:T(8,128)(2,1)S(1)}, bf16[128,768]{1,0:T(8,128)(2,1)S(1)}, u32[]{:S(2)}, u32[]{:S(2)}) collective-permute-start(bf16[128,768]{1,0:T(8,128)(2,1)S(1)} %get-tuple-element.137.refs_0_), channel_id=1, source_target_pairs={{0,2},{1,3},{2,0},{3,1},{4,6},{5,7},{6,4},{7,5},{8,10},{9,11},{10,... | collective-permute-start | bytes 589832 | tf_op jit(solution)/shard_map/ppermute | solution.py:1094
  115.8 7.0 %collective-permute-start.19 = (bf16[128,768]{1,0:T(8,128)(2,1)S(1)}, bf16[128,768]{1,0:T(8,128)(2,1)S(1)}, u32[]{:S(2)}, u32[]{:S(2)}) collective-permute-start(bf16[128,768]{1,0:T(8,128)(2,1)S(1)} %get-tuple-element.137.refs_0_), channel_id=1, source_target_pairs={{0,1},{1,0},{2,3},{3,2},{4,5},{5,4},{6,7},{7,6},{8,9},{9,8},{10,11... | collective-permute-start | bytes 589832 | tf_op jit(solution)/shard_map/ppermute | solution.py:1091
  122.4 1.4 collective-permute-start.20
  122.4 12.4 %collective-permute-start.24 = (bf16[2,128,768]{2,1,0:T(8,128)(2,1)S(1)}, bf16[2,128,768]{2,1,0:T(8,128)(2,1)S(1)}, u32[]{:S(2)}, u32[]{:S(2)}) collective-permute-start(bf16[2,128,768]{2,1,0:T(8,128)(2,1)S(1)} %get-tuple-element.145.refs_0_), channel_id=1, source_target_pairs={{0,2},{1,3},{2,0},{3,1},{4,6},{5,7},{6,4},{7,5},{8,10},{9,11},{10,... | collective-permute-start | bytes 1179656 | tf_op jit(solution)/shard_map/ppermute | solution.py:1094
  134.2 1.8 collective-permute-start.21
  134.4 2.4 collective-permute-start.23
  134.8 2.3 collective-permute-start.25
  136.1 11.2 %collective-permute-start.22 = (bf16[256,768]{1,0:T(8,128)(2,1)S(1)}, bf16[256,768]{1,0:T(8,128)(2,1)S(1)}, u32[]{:S(2)}, u32[]{:S(2)}) collective-permute-start(bf16[256,768]{1,0:T(8,128)(2,1)S(1)} %add_convert_fusion.2.refs_2_), channel_id=1, source_target_pairs={{0,2},{1,3},{2,0},{3,1},{4,6},{5,7},{6,4},{7,5},{8,10},{9,11},{10,... | collective-permute-start | bytes 1179656 | tf_op jit(solution)/shard_map/ppermute | solution.py:1094
  148.8 4.3 %collective-permute-start.26 = (bf16[256,768]{1,0:T(8,128)(2,1)S(1)}, bf16[256,768]{1,0:T(8,128)(2,1)S(1)}, u32[]{:S(2)}, u32[]{:S(2)}) collective-permute-start(bf16[256,768]{1,0:T(8,128)(2,1)S(1)} %get-tuple-element.149.refs_13_.refs_0_), channel_id=1, source_target_pairs={{0,1},{1,0},{2,3},{3,2},{4,5},{5,4},{6,7},{7,6},{8,9},{9,8},{10,11... | collective-permute-start | bytes 1179656 | tf_op jit(solution)/shard_map/ppermute | solution.py:1091
  150.9 35.2 %collective-permute-start.30 = (bf16[2,416,768]{2,1,0:T(8,128)(2,1)S(1)}, bf16[2,416,768]{2,1,0:T(8,128)(2,1)S(1)}, u32[]{:S(2)}, u32[]{:S(2)}) collective-permute-start(bf16[2,416,768]{2,1,0:T(8,128)(2,1)S(1)} %get-tuple-element.152), channel_id=1, source_target_pairs={{0,1},{1,0},{2,3},{3,2},{4,5},{5,4},{6,7},{7,6},{8,9},{9,8},{10,11... | collective-permute-start | bytes 3833864 | tf_op jit(solution)/shard_map/ppermute | solution.py:1091
  151.5 28.0 %collective-permute-start.32 = (bf16[384,1536]{1,0:T(8,128)(2,1)S(1)}, bf16[384,1536]{1,0:T(8,128)(2,1)S(1)}, u32[]{:S(2)}, u32[]{:S(2)}) collective-permute-start(bf16[384,1536]{1,0:T(8,128)(2,1)S(1)} %get-tuple-element.172), channel_id=1, source_target_pairs={{0,8},{4,12},{8,0},{12,4},{16,24},{20,28},{24,16},{28,20},{1,9},{5... | collective-permute-start | bytes 3538952 | tf_op jit(solution)/shard_map/ppermute | solution.py:1121
  162.3 2.3 collective-permute-start.27
  162.3 22.5 %collective-permute-start.33 = (bf16[432,960]{1,0:T(8,128)(2,1)S(1)}, bf16[432,960]{1,0:T(8,128)(2,1)S(1)}, u32[]{:S(2)}, u32[]{:S(2)}) collective-permute-start(bf16[432,960]{1,0:T(8,128)(2,1)S(1)} %get-tuple-element.176), channel_id=1, source_target_pairs={{0,4},{4,0},{8,12},{12,8},{16,20},{20,16},{24,28},{28,24},{1,5},{5... | collective-permute-start | bytes 2488328 | tf_op jit(solution)/shard_map/ppermute | solution.py:1121
  163.9 32.3 %collective-permute-start.34 = (bf16[432,576]{1,0:T(8,128)(2,1)S(1)}, bf16[432,576]{1,0:T(8,128)(2,1)S(1)}, u32[]{:S(2)}, u32[]{:S(2)}) collective-permute-start(bf16[432,576]{1,0:T(8,128)(2,1)S(1)} %get-tuple-element.180), channel_id=1, source_target_pairs={{0,4},{4,0},{8,12},{12,8},{16,20},{20,16},{24,28},{28,24},{1,5},{5... | collective-permute-start | bytes 1493000 | tf_op jit(solution)/shard_map/ppermute | solution.py:1121
  164.7 54.2 %collective-permute-start.28 = (bf16[512,768]{1,0:T(8,128)(2,1)S(1)}, bf16[512,768]{1,0:T(8,128)(2,1)S(1)}, u32[]{:S(2)}, u32[]{:S(2)}) collective-permute-start(bf16[512,768]{1,0:T(8,128)(2,1)S(1)} %pad_maximum_fusion), channel_id=1, source_target_pairs={{0,2},{1,3},{2,0},{3,1},{4,6},{5,7},{6,4},{7,5},{8,10},{9,11},{10,... | collective-permute-start | bytes 2359304 | tf_op jit(solution)/shard_map/ppermute | solution.py:1094
  180.2 28.2 %collective-permute-start.35 = (bf16[192,1536]{1,0:T(8,128)(2,1)S(1)}, bf16[192,1536]{1,0:T(8,128)(2,1)S(1)}, u32[]{:S(2)}, u32[]{:S(2)}) collective-permute-start(bf16[192,1536]{1,0:T(8,128)(2,1)S(1)} %get-tuple-element.173), channel_id=1, source_target_pairs={{0,16},{4,20},{8,24},{12,28},{16,0},{20,4},{24,8},{28,12},{1,17},{... | collective-permute-start | bytes 1769480 | tf_op jit(solution)/shard_map/ppermute | solution.py:1121
  185.6 25.0 %collective-permute-start.36 = (bf16[240,960]{1,0:T(8,128)(2,1)S(1)}, bf16[240,960]{1,0:T(8,128)(2,1)S(1)}, u32[]{:S(2)}, u32[]{:S(2)}) collective-permute-start(bf16[240,960]{1,0:T(8,128)(2,1)S(1)} %get-tuple-element.177), channel_id=1, source_target_pairs={{0,8},{4,12},{8,0},{12,4},{16,24},{20,28},{24,16},{28,20},{1,9},{5... | collective-permute-start | bytes 1382408 | tf_op jit(solution)/shard_map/ppermute | solution.py:1121
  186.3 35.7 %collective-permute-start.31 = (bf16[416,768]{1,0:T(8,128)(2,1)S(1)}, bf16[416,768]{1,0:T(8,128)(2,1)S(1)}, u32[]{:S(2)}, u32[]{:S(2)}) collective-permute-start(bf16[416,768]{1,0:T(8,128)(2,1)S(1)} %fusion.1), channel_id=1, source_target_pairs={{0,2},{1,3},{2,0},{3,1},{4,6},{5,7},{6,4},{7,5},{8,10},{9,11},{10,... | collective-permute-start | bytes 1916936 | tf_op jit(solution)/shard_map/ppermute | solution.py:1094
  197.0 21.2 %collective-permute-start.37 = (bf16[240,576]{1,0:T(8,128)(2,1)S(1)}, bf16[240,576]{1,0:T(8,128)(2,1)S(1)}, u32[]{:S(2)}, u32[]{:S(2)}) collective-permute-start(bf16[240,576]{1,0:T(8,128)(2,1)S(1)} %get-tuple-element.181), channel_id=1, source_target_pairs={{0,8},{4,12},{8,0},{12,4},{16,24},{20,28},{24,16},{28,20},{1,9},{5... | collective-permute-start | bytes 829448 | tf_op jit(solution)/shard_map/ppermute | solution.py:1121
  209.1 11.5 %collective-permute-start.38 = (bf16[96,1536]{1,0:T(8,128)(2,1)S(1)}, bf16[96,1536]{1,0:T(8,128)(2,1)S(1)}, u32[]{:S(2)}, u32[]{:S(2)}) collective-permute-start(bf16[96,1536]{1,0:T(8,128)(2,1)S(1)} %get-tuple-element.184), channel_id=1, source_target_pairs={{0,4},{4,0},{8,12},{12,8},{16,20},{20,16},{24,28},{28,24},{1,5},{5... | collective-permute-start | bytes 884744 | tf_op jit(solution)/shard_map/ppermute | solution.py:1121
  211.3 20.8 %collective-permute-start.39 = (bf16[144,960]{1,0:T(8,128)(2,1)S(1)}, bf16[144,960]{1,0:T(8,128)(2,1)S(1)}, u32[]{:S(2)}, u32[]{:S(2)}) collective-permute-start(bf16[144,960]{1,0:T(8,128)(2,1)S(1)} %get-tuple-element.188), channel_id=1, source_target_pairs={{0,16},{4,20},{8,24},{12,28},{16,0},{20,4},{24,8},{28,12},{1,17},{... | collective-permute-start | bytes 829448 | tf_op jit(solution)/shard_map/ppermute | solution.py:1121
  218.8 15.5 %collective-permute-start.40 = (bf16[144,576]{1,0:T(8,128)(2,1)S(1)}, bf16[144,576]{1,0:T(8,128)(2,1)S(1)}, u32[]{:S(2)}, u32[]{:S(2)}) collective-permute-start(bf16[144,576]{1,0:T(8,128)(2,1)S(1)} %get-tuple-element.192), channel_id=1, source_target_pairs={{0,16},{4,20},{8,24},{12,28},{16,0},{20,4},{24,8},{28,12},{1,17},{... | collective-permute-start | bytes 497672 | tf_op jit(solution)/shard_map/ppermute | solution.py:1121
  219.0 22.8 %collective-permute-start.29 = (f32[256,768]{1,0:T(8,128)S(1)}, f32[256,768]{1,0:T(8,128)S(1)}, u32[]{:S(2)}, u32[]{:S(2)}) collective-permute-start(f32[256,768]{1,0:T(8,128)S(1)} %add_add_fusion.refs_0_), channel_id=1, source_target_pairs={{0,1},{1,0},{2,3},{3,2},{4,5},{5,4},{6,7},{7,6},{8,9},{9,8},{10,11... | collective-permute-start | bytes 2359304 | tf_op jit(solution)/shard_map/ppermute | solution.py:1091
  233.6 2.1 collective-permute-start.41
  235.7 4.2 %collective-permute-start.42 = (f32[16,768]{1,0:T(8,128)S(1)}, f32[16,768]{1,0:T(8,128)S(1)}, u32[]{:S(2)}, u32[]{:S(2)}) collective-permute-start(f32[16,768]{1,0:T(8,128)S(1)} %add.74), channel_id=1, source_target_pairs={{0,2},{1,3},{2,0},{3,1},{4,6},{5,7},{6,4},{7,5},{8,10},{9,11},{10,... | collective-permute-start | bytes 147464 | tf_op jit(solution)/shard_map/ppermute | solution.py:1048
  (53 other events, 408.1 us)
where the time goes:
time: 248 us; the launch traced here: 244 us
  waiting for transfers between devices  102 us (41%)
  Pallas kernels  89.2 us (36%)
  starting transfers between devices  27.2 us (11%)
  local copies, waits for them, and re-layouts  18.8 us (8%)
  other arithmetic  4.27 us (2%)
  between operations  2.97 us (1%)
    pallas_call x24, Pallas kernels, launch(): pl.pallas_call(kernel, in_specs=in_specs, out_specs=out_specs, out_shape=...  89.2 us
    ppermute x11, waiting for transfers between devices, on_device(): over = lambda v, bit: lax.ppermute(v, 'wide', flip(bit, wide))  74.6 us
    ppermute x10, waiting for transfers between devices, to_across(): return lax.ppermute(v, 'narrow', ACROSS)  19.1 us
    ppermute x11, starting transfers between devices, on_device(): over = lambda v, bit: lax.ppermute(v, 'wide', flip(bit, wide))  12.8 us
    unnamed x116, local copies, waits for them, and re-layouts  12.3 us
    ppermute x10, starting transfers between devices, to_across(): return lax.ppermute(v, 'narrow', ACROSS)  9.66 us
    ppermute x20, waiting for transfers between devices, to_core(): return lax.ppermute(v, 'narrow', CORE)  5.88 us
  transfers between devices with their start and end apart: 43, of which 18 were waited for; matrix products, arithmetic and copies ran while one was open for 4% of the time, Pallas kernels for 28%

commit v1 on v0

--- a/solution.py
+++ b/solution.py
@@ -13,7 +13,7 @@
 NT = (((1,), (1,)), ((), ()))
 TN = (((0,), (0,)), ((), ()))
 EPS = 1e-05
-PACE = 1.1e8
+PACE = 1.1e7
 SELF_MIB = 60
 EXTRA = 16
 
@@ -407,8 +407,13 @@
     )[0]
 
 
-def keys_values(at, shards, w, nh):
-    seg, width = shards[0].shape
+def shard_views(pairs):
+    view = lambda flips: lambda ref, at: ref.at[at[1] ^ flips]
+    return [near(pairs[0], view(0)), near(pairs[1], view(0)), near(pairs[0], view(1)), near(pairs[1], view(1))]
+
+
+def keys_values(at, pairs, w, nh):
+    _, seg, width = pairs[0].shape
     local = w.shape[1]
     hd = local // nh
 
@@ -425,7 +430,7 @@
                     out[h, span, :] = jnp.concatenate([high[:, part], low[:, part]], axis=1)
 
     out = shape(nh, 4 * seg, 2 * hd, dtype=BF)
-    return launch(body, "keys_values", at, [near(s) for s in shards] + [near(w)], [out, out], us=2)
+    return launch(body, "keys_values", at, shard_views(pairs) + [near(w)], [out, out], us=2)
 
 
 def cross_forward(at, mine, other, bias_mine, bias_other, keys, values, w, b, wo, nh):
@@ -784,11 +789,11 @@
     )
 
 
-def cross_grads(at, z_blocks, mine, other, dquery, heads, shards, dkv, first_mine, first_other, flat, small, nh, blocks):
+def cross_grads(at, z_blocks, mine, other, dquery, heads, pairs, dkv, first_mine, first_other, flat, small, nh, blocks):
     half, width = mine.shape
     local = dquery.shape[1]
     hd = local // nh
-    seg = shards[0].shape[0]
+    seg = pairs[0].shape[1]
     feed_sums, first_sums, fc1_sum, head_sums = small
 
     def body(at, ins, outs, scratch):
@@ -826,11 +831,11 @@
         body,
         "cross_grads",
         at,
-        [
+        [near(z) for z in z_blocks]
+        + shard_views(pairs)
+        + [
             near(a)
             for a in (
-                *z_blocks,
-                *shards,
                 mine,
                 other,
                 dquery,
@@ -1100,7 +1105,14 @@
     def chip_sum(keep, send):
         return (keep + to_core(send).astype(F32)).astype(BF)
 
-    store_x = to_across(store[0])
+    def gather_pair(v, groups):
+        return lax.all_gather(v, "narrow", axis=0, axis_index_groups=groups)
+
+    by_x, by_core = [[0, 2], [1, 3]], [[0, 1], [2, 3]]
+    share = lambda v: lax.dynamic_slice_in_dim(v, doc % 2 * (v.shape[0] // 2), v.shape[0] // 2, 0)
+    over = lambda v, bit: lax.ppermute(v, "wide", flip(bit, wide))
+    store_pair = gather_pair(store[0], by_x)
+    f2_pair = gather_pair(share(fc2_weight), by_x)
     qkv, prob, flat, send, keep = self_forward(
         at, tokens, self_w, self_qv_bias, self_out_weight, row(fc1_bias), nh
     )
@@ -1116,23 +1128,21 @@
     )
     terms_close = close
     other = to_across(mine)
-    doc_bit = doc % 2
-    share = lambda v: lax.dynamic_slice_in_dim(v, doc_bit * (v.shape[0] // 2), v.shape[0] // 2, 0)
-    over = lambda v, bit: lax.ppermute(v, "wide", flip(bit, wide))
-    f1_half, f2_half = tie((share(fc1_weight), share(fc2_weight)), mine)
-    f1_x, f2_x = to_across(f1_half), to_across(f2_half)
     index = index_rows(top_index)
-    bias_mine = make_mask(tie(at, mine, f1_half, f2_half), index, top_index.shape, seg, 128, 0)
-    store_x = tie(store_x, bias_mine)
-    shards = [store[0], to_core(tie(store[0], bias_mine)), store_x, to_core(store_x)]
-    bias_other = make_mask(tie(at, bias_mine), index, top_index.shape, seg, 128, 1)
-    other, f1_x = tie((other, f1_x), bias_other)
-    f1_y = over(f1_x, 1)
+    bias_mine = make_mask(tie(at, mine), index, top_index.shape, seg, 128, 0)
+    other = tie(other, bias_mine)
+    f1_half = share(tie(fc1_weight, bias_mine))
+    f1_x = to_across(f1_half)
     first_total, after, after_low = first_norm(at, mine, other, tokens, row(self_out_bias), norm_gain, norm_shift)
     after_other = to_core(after_low)
-
-    keys, values = keys_values(tie(at, after_low), shards, cross_w, nh)
-    f1_core = to_core(tie(fc1_weight, keys))
+    f1_core, f2_core = to_core(tie(fc1_weight, after_low)), to_core(tie(fc2_weight, after_low))
+    bias_other = make_mask(tie(at, after_low, f1_half), index, top_index.shape, seg, 128, 1)
+    store_pair = tie(store_pair, other)
+    pairs = (store_pair, to_core(store_pair))
+    f1_x, after_other, f1_core, f2_core = tie((f1_x, after_other, f1_core, f2_core), bias_other)
+    f1_y, f1_xc = over(f1_x, 1), to_core(f1_x)
+
+    keys, values = keys_values(tie(at, bias_other), pairs, cross_w, nh)
     keep, send, raised, inverse, query, heads = cross_forward(
         tie(at, keys), after_low, after_other, bias_mine, bias_other, keys, values, cross_w, qv_bias, out_weight, nh
     )
@@ -1144,14 +1154,13 @@
             + lax.dynamic_slice_in_dim(close, theirs, quarter, 0).astype(F32)
         ).astype(BF)
     )
-    f2_x = tie(f2_x, keep)
-    f2_y = over(f2_x, 1)
-    f2_core = to_core(tie(fc2_weight, keep))
+    f2_x = lax.dynamic_index_in_dim(tie(f2_pair, keep), 1 - across, 0, keepdims=False)
+    f2_y, f2_xc = over(f2_x, 1), to_core(f2_x)
     f1_y = tie(f1_y, close)
     f2_y = tie(f2_y, distant)
     weights = (
-        (fc1_weight, f1_core, f1_x, f1_y, to_core(f1_x), to_core(f1_y)),
-        (fc2_weight, f2_core, f2_x, f2_y, to_core(f2_x), to_core(f2_y)),
+        (fc1_weight, f1_core, f1_x, f1_y, f1_xc, to_core(f1_y)),
+        (fc2_weight, f2_core, f2_x, f2_y, f2_xc, to_core(f2_y)),
     )
 
     pair, mixed_own, z, feed_sums = feed(
@@ -1190,7 +1199,7 @@
         after_other,
         dquery,
         heads,
-        shards,
+        pairs,
         dkv,
         dfirst_low,
         dfirst_other,

time: 248 us -> 270 us (1.089)
  waiting for transfers between devices: 102 us -> 86.6 us
  local copies, waits for them, and re-layouts: 18.8 us -> 34.1 us
  between operations: 2.97 us -> 16 us
  starting transfers between devices: 27.2 us -> 32.4 us
  Pallas kernels: 89.2 us -> 92.8 us
    ppermute x11, waiting for transfers between devices: 74.6 us -> 58.4 us  [on_device(): over = lambda v, bit: lax.ppermute(v, 'wide', flip(bit, wide))]
    unnamed x116 -> x96, local copies, waits for them, and re-layouts: 12.3 us -> 22.9 us
    ppermute x10 -> x8, starting transfers between devices: 9.66 us -> 15.7 us  [to_across(): return lax.ppermute(v, 'narrow', ACROSS)]
    all_gather x0 -> x2, waiting for transfers between devices: none -> 4.47 us  [gather_pair(): return lax.all_gather(v, 'narrow', axis=0, axis_index_groups=groups)]
    pallas_call x24, Pallas kernels: 89.2 us -> 92.8 us  [launch(): pl.pallas_call(kernel, in_specs=in_specs, out_specs=out_specs, out_shape=...]
    ppermute x10 -> x8, waiting for transfers between devices: 19.1 us -> 17 us  [to_across(): return lax.ppermute(v, 'narrow', ACROSS)]
    ppermute x20 -> x19, waiting for transfers between devices: 5.88 us -> 5.13 us  [to_core(): return lax.ppermute(v, 'narrow', CORE)]
  transfers between devices with their start and end apart: 43 -> 42, of which waited for: 18 -> 18; matrix products, arithmetic and copies ran while one was open for 4% -> 5% of each run, Pallas kernels for 28% -> 27%
where the time goes in v1:
time: 270 us; the launch traced here: 267 us
  Pallas kernels  92.8 us (34%)
  waiting for transfers between devices  86.6 us (32%)
  local copies, waits for them, and re-layouts  34.1 us (13%)
  starting transfers between devices  32.4 us (12%)
  between operations  16 us (6%)
  other arithmetic  4.84 us (2%)
    pallas_call x24, Pallas kernels, launch(): pl.pallas_call(kernel, in_specs=in_specs, out_specs=out_specs, out_shape=...  92.8 us
    ppermute x11, waiting for transfers between devices, on_device(): over = lambda v, bit: lax.ppermute(v, 'wide', flip(bit, wide))  58.4 us
    unnamed x96, local copies, waits for them, and re-layouts  22.9 us
    ppermute x8, waiting for transfers between devices, to_across(): return lax.ppermute(v, 'narrow', ACROSS)  17 us
    ppermute x8, starting transfers between devices, to_across(): return lax.ppermute(v, 'narrow', ACROSS)  15.7 us
    ppermute x11, starting transfers between devices, on_device(): over = lambda v, bit: lax.ppermute(v, 'wide', flip(bit, wide))  11.6 us
  transfers between devices with their start and end apart: 42, of which 18 were waited for; matrix products, arithmetic and copies ran while one was open for 5% of the time, Pallas kernels for 27%

profile of v1, /device:TPU:0, one launch (start us, length us, event | category | flops | bytes accessed | tf_op | source)
XLA Modules:
  0.0 266.7 jit_solution(2497273015125759557)
XLA Ops:
  9.8 7.5 %self_fwd.1 = (bf16[3,512,192]{2,1,0:T(8,128)(2,1)}, bf16[3,512,512]{2,1,0:T(8,128)(2,1)}, bf16[512,192]{1,0:T(8,128)(2,1)}, bf16[272,768]{1,0:T(8,128)(2,1)}, f32[256,768]{1,0:T(8,128)}) custom-call(s32[7]{0:T(128)} %stack.33.at_ref, bf16[512,768]{1,0:T(8,128)(2,1)} %refs_5_.7, bf16[3,192,768]{2,1,0:T(8,128)(2,1)} %bitcast.33, bf16[192,768]{1,0:T(8,128)(2,1)} %refs_2_.5, ...), custom_call_target="tpu_custom_call" | custom-call | flops 44000000 | bytes 1000 | tf_op jit(solution)/shard_map/self_fwd/pallas_call | solution.py:160
  21.6 2.9 %collective-permute-start.1 = (bf16[272,768]{1,0:T(8,128)(2,1)S(1)}, bf16[272,768]{1,0:T(8,128)(2,1)S(1)}, u32[]{:S(2)}, u32[]{:S(2)}) collective-permute-start(bf16[272,768]{1,0:T(8,128)(2,1)S(1)} %maximum_maximum_fusion.refs_0_), channel_id=1, source_target_pairs={{0,2},{1,3},{2,0},{3,1},{4,6},{5,7},{6,4},{7,5},{8,10},{9,11},{10,... | collective-permute-start | bytes 1253384 | tf_op jit(solution)/shard_map/ppermute | solution.py:1099
  24.5 3.0 %copy-done = s32[512,3,4,256]{3,2,1,0:T(4,128)S(1)} copy-done((s32[512,3,4,256]{3,2,1,0:T(4,128)S(1)}, s32[512,3,4,256]{3,2,1,0:T(4,128)}, u32[]{:S(2)}) %copy-start) | copy-done | bytes 6291480
  27.6 9.6 %mask.2.refs_4_ = bf16[3,256,1664]{2,1,0:T(8,128)(2,1)S(1)} custom-call(s32[7]{0:T(128)S(1)} %copy-done.32, s32[4,3072,128]{2,1,0:T(8,128)S(1)} %bitcast.25), custom_call_target="tpu_custom_call" | custom-call | flops 110000000 | bytes 1000 | tf_op jit(solution)/shard_map/mask/pallas_call | solution.py:160
  37.2 1.4 copy-done.4
  39.9 1.7 first_norm.1
  43.9 4.5 %all-gather.4.cloned.1.call-done.refs_0_.refs_2_.refs_4_.refs_6_ = bf16[2,416,768]{2,1,0:T(8,128)(2,1)} async-done(((bf16[1,416,768]{2,1,0:T(8,128)(2,1)}), bf16[2,416,768]{2,1,0:T(8,128)(2,1)}) %all-gather.4.cloned.1.call-update) | async-done | bytes 1277968 | tf_op jit(solution)/shard_map/all_gather | solution.py:1109
  48.4 2.0 constant_dynamic-slice_fusion
  50.4 1.9 constant_dynamic-slice_fusion.1
  52.3 1.7 collective-permute-start.3
  54.3 2.8 %copy-done.1 = s32[512,3,4,256]{3,2,1,0:T(4,128)S(1)} copy-done((s32[512,3,4,256]{3,2,1,0:T(4,128)S(1)}, s32[512,3,4,256]{3,2,1,0:T(4,128)}, u32[]{:S(2)}) %copy-start.1) | copy-done | bytes 6291480
  57.0 9.6 %mask.3.refs_5_ = bf16[3,256,1664]{2,1,0:T(8,128)(2,1)S(1)} custom-call(s32[7]{0:T(128)S(1)} %copy-done.32, s32[4,3072,128]{2,1,0:T(8,128)S(1)} %bitcast.26), custom_call_target="tpu_custom_call" | custom-call | flops 110000000 | bytes 1000 | tf_op jit(solution)/shard_map/mask/pallas_call | solution.py:160
  66.7 8.8 %collective-permute-done.3.refs_14_ = bf16[384,768]{1,0:T(8,128)(2,1)} collective-permute-done((bf16[384,768]{1,0:T(8,128)(2,1)}, bf16[384,768]{1,0:T(8,128)(2,1)}, u32[]{:S(2)}, u32[]{:S(2)}) %collective-permute-start.3) | collective-permute-done | bytes 589856 | tf_op jit(solution)/shard_map/ppermute | solution.py:1099
  75.5 1.4 collective-permute-start.9
  77.0 2.2 keys_values.1
  79.3 8.1 %cross_fwd.1 = (f32[256,768]{1,0:T(8,128)S(1)}, bf16[256,768]{1,0:T(8,128)(2,1)S(1)}, bf16[3,512,1664]{2,1,0:T(8,128)(2,1)S(1)}, f32[3,512,128]{2,1,0:T(8,128)S(...) custom-call(s32[7]{0:T(128)S(1)} %copy-done.32, bf16[256,768]{1,0:T(8,128)(2,1)} %get-tuple-element.119.refs_0_.refs_8_, ...), custom_call_target="tpu_custom_call" | custom-call | flops 99000000 | bytes 1000 | tf_op jit(solution)/shard_map/cross_fwd/pallas_call | solution.py:160
  87.4 2.3 copy-done.8
  95.9 2.0 dynamic-slice_bitcast_fusion.refs_20_
  99.6 2.6 collective-permute-start.8
  102.7 11.2 %collective-permute-done.12.refs_21_ = bf16[384,768]{1,0:T(8,128)(2,1)} collective-permute-done((bf16[384,768]{1,0:T(8,128)(2,1)}, bf16[384,768]{1,0:T(8,128)(2,1)}, u32[]{:S(2)}, u32[]{:S(2)}) %collective-permute-start.12) | collective-permute-done | bytes 589856 | tf_op jit(solution)/shard_map/ppermute | solution.py:1113
  114.0 2.1 collective-permute-done.14.refs_23_
  120.8 10.7 %feed.1 = (bf16[2,128,768]{2,1,0:T(8,128)(2,1)S(1)}, bf16[128,768]{1,0:T(8,128)(2,1)S(1)}, bf16[128,768]{1,0:T(8,128)(2,1)S(1)}, f32[8,768]{1,0:T(8,128)S(1)}) custom-call(s32[7]{0:T(128)S(1)} %copy-done.32, f32[256,768]{1,0:T(8,128)S(1)} %copy-done.29, f32[256,768]{1,0:T(8,128)S(1)} %copy-done.15, bf16[256,768]{1,0:T(8,128)(2,1)} %collective-permute-done.7.refs_2_, ...), custom_call_target="tpu_custom_call" | custom-call | flops 110000000 | bytes 1000 | tf_op jit(solution)/shard_map/feed/pallas_call | solution.py:160
  131.5 2.5 collective-permute-start.15
  134.0 5.2 %collective-permute-done.15.refs_2_.refs_1_ = bf16[128,768]{1,0:T(8,128)(2,1)S(1)} collective-permute-done((bf16[128,768]{1,0:T(8,128)(2,1)S(1)}, bf16[128,768]{1,0:T(8,128)(2,1)S(1)}, u32[]{:S(2)}, u32[]{:S(2)}) %collective-permute-start.15) | collective-permute-done | bytes 196640 | tf_op jit(solution)/shard_map/ppermute | solution.py:1099
  139.2 1.7 collective-permute-start.21
  141.0 10.4 %cross_bwd.1 = (f32[256,768]{1,0:T(8,128)S(1)}, bf16[256,768]{1,0:T(8,128)(2,1)S(1)}, bf16[512,192]{1,0:T(8,128)(2,1)S(1)}, bf16[3,1664,128]{2,1,0:T(8,128)(2,1)S(1)}, f32[2,192]{1,0:T(2,128)S(1)}) custom-call(s32[7]{0:T(128)S(1)} %copy-done.32, bf16[128,768]{1,0:T(8,128)(2,1)S(1)} %get-tuple-element.139.refs_0_, ...), custom_call_target="tpu_custom_call" | custom-call | flops 121000000 | bytes 1000 | tf_op jit(solution)/shard_map/cross_bwd/pallas_call | solution.py:160
  153.2 1.5 collective-permute-start.19
  154.7 8.1 %feed_grads.1 = (bf16[384,1536]{1,0:T(8,128)(2,1)S(1)}, f32[4,96,1536]{2,1,0:T(8,128)S(1)}, f32[1,768]{1,0:T(1,128)S(1)}) custom-call(s32[7]{0:T(128)S(1)} %copy-done.32, bf16[2,128,768]{2,1,0:T(8,128)(2,1)S(1)} %get-tuple-element.147.refs_0_, bf16[2,128,768]{2,1,0:T(8,128)(2,1)S(1)} %collective-permute-done.20.refs_1_, ...), custom_call_target="tpu_custom_call" | custom-call | flops 66000000 | bytes 1000 | tf_op jit(solution)/shard_map/feed_grads/pallas_call | solution.py:160
  162.8 1.8 collective-permute-done.19.refs_3_
  166.0 2.1 store_grad.1
  168.7 1.7 collective-permute-start.29
  170.4 4.6 %cross_grads.1 = (bf16[432,960]{1,0:T(8,128)(2,1)S(1)}, f32[4,96,960]{2,1,0:T(8,128)S(1)}, f32[16,768]{1,0:T(8,128)S(1)}) custom-call(s32[7]{0:T(128)S(1)} %copy-done.32, bf16[128,768]{1,0:T(8,128)(2,1)S(1)} %get-tuple-element.139.refs_0_, bf16[128,768]{1,0:T(8,128)(2,1)S(1)} %collective-permute-done.16.refs_1_, ...), custom_call_target="tpu_custom_call" | custom-call | flops 44000000 | bytes 1000 | tf_op jit(solution)/shard_map/cross_grads/pallas_call | solution.py:160
  175.0 5.1 %self_bwd.1 = (bf16[384,768]{1,0:T(8,128)(2,1)S(1)}, f32[256,768]{1,0:T(8,128)S(1)}, bf16[432,576]{1,0:T(8,128)(2,1)S(1)}, f32[4,96,576]{2,1,0:T(8,128)S(1)}, f32[16,576]{1,0:T(8,128)S(1)}) custom-call(s32[7]{0:T(128)S(1)} %copy-done.32, bf16[256,768]{1,0:T(8,128)(2,1)S(1)} %get-tuple-element.151.refs_13_.refs_0_, ...), custom_call_target="tpu_custom_call" | custom-call | flops 66000000 | bytes 1000 | tf_op jit(solution)/shard_map/self_bwd/pallas_call | solution.py:160
  180.7 1.4 collective-permute-done.24.refs_1_
  184.2 12.4 %collective-permute-done.29.refs_1_ = bf16[384,1536]{1,0:T(8,128)(2,1)S(1)} collective-permute-done((bf16[384,1536]{1,0:T(8,128)(2,1)S(1)}, bf16[384,1536]{1,0:T(8,128)(2,1)S(1)}, u32[]{:S(2)}, u32[]{:S(2)}) %collective-permute-start.29) | collective-permute-done | bytes 1179680 | tf_op jit(solution)/shard_map/ppermute | solution.py:1113
  197.4 2.8 %collective-permute-start.32 = (bf16[192,1536]{1,0:T(8,128)(2,1)S(1)}, bf16[192,1536]{1,0:T(8,128)(2,1)S(1)}, u32[]{:S(2)}, u32[]{:S(2)}) collective-permute-start(bf16[192,1536]{1,0:T(8,128)(2,1)S(1)} %get-tuple-element.175), channel_id=1, source_target_pairs={{0,16},{4,20},{8,24},{12,28},{16,0},{20,4},{24,8},{28,12},{1,17},{... | collective-permute-start | bytes 1769480 | tf_op jit(solution)/shard_map/ppermute | solution.py:1113
  200.3 2.4 collective-permute-done.30.refs_1_
  205.4 8.7 %collective-permute-done.31.refs_1_ = bf16[432,576]{1,0:T(8,128)(2,1)S(1)} collective-permute-done((bf16[432,576]{1,0:T(8,128)(2,1)S(1)}, bf16[432,576]{1,0:T(8,128)(2,1)S(1)}, u32[]{:S(2)}, u32[]{:S(2)}) %collective-permute-start.31) | collective-permute-done | bytes 497696 | tf_op jit(solution)/shard_map/ppermute | solution.py:1113
  215.2 10.5 %collective-permute-done.32.refs_1_ = bf16[192,1536]{1,0:T(8,128)(2,1)S(1)} collective-permute-done((bf16[192,1536]{1,0:T(8,128)(2,1)S(1)}, bf16[192,1536]{1,0:T(8,128)(2,1)S(1)}, u32[]{:S(2)}, u32[]{:S(2)}) %collective-permute-start.32) | collective-permute-done | bytes 589856 | tf_op jit(solution)/shard_map/ppermute | solution.py:1113
  227.1 1.7 collective-permute-done.33.refs_1_
  229.5 2.0 collective-permute-start.36
  231.4 4.4 %collective-permute-done.34.refs_1_ = bf16[240,576]{1,0:T(8,128)(2,1)S(1)} collective-permute-done((bf16[240,576]{1,0:T(8,128)(2,1)S(1)}, bf16[240,576]{1,0:T(8,128)(2,1)S(1)}, u32[]{:S(2)}, u32[]{:S(2)}) %collective-permute-start.34) | collective-permute-done | bytes 276512 | tf_op jit(solution)/shard_map/ppermute | solution.py:1113
  237.2 1.5 join_quarters.1
  238.7 1.4 last_stage.3
  241.4 7.1 %collective-permute-done.36.refs_1_ = bf16[144,960]{1,0:T(8,128)(2,1)S(1)} collective-permute-done((bf16[144,960]{1,0:T(8,128)(2,1)S(1)}, bf16[144,960]{1,0:T(8,128)(2,1)S(1)}, u32[]{:S(2)}, u32[]{:S(2)}) %collective-permute-start.36) | collective-permute-done | bytes 276512 | tf_op jit(solution)/shard_map/ppermute | solution.py:1113
  248.5 1.5 last_stage.4
  254.9 1.5 collective-permute-done.39
  257.6 1.8 join_halves.1
  (191 shorter events, 44.9 us)
Async XLA Ops:
  7.2 41.2 %all-gather.4.cloned.1.call-start = ((), (), s32[]{:S(2)}) async-start(), calls=%async_computation | async-start | bytes 1916928 | tf_op jit(solution)/shard_map/all_gather | solution.py:1109
  17.3 2.1 collective-permute-start
  17.9 77.9 %all-gather.6.cloned.1.call-start = ((), (), s32[]{:S(2)}) async-start(), calls=%async_computation.1 | async-start | bytes 1769472 | tf_op jit(solution)/shard_map/all_gather | solution.py:1109
  21.6 18.3 %collective-permute-start.1 = (bf16[272,768]{1,0:T(8,128)(2,1)S(1)}, bf16[272,768]{1,0:T(8,128)(2,1)S(1)}, u32[]{:S(2)}, u32[]{:S(2)}) collective-permute-start(bf16[272,768]{1,0:T(8,128)(2,1)S(1)} %maximum_maximum_fusion.refs_0_), channel_id=1, source_target_pairs={{0,2},{1,3},{2,0},{3,1},{4,6},{5,7},{6,4},{7,5},{8,10},{9,11},{10,... | collective-permute-start | bytes 1253384 | tf_op jit(solution)/shard_map/ppermute | solution.py:1099
  43.4 32.1 %collective-permute-start.5 = (bf16[768,768]{1,0:T(8,128)(2,1)}, bf16[768,768]{1,0:T(8,128)(2,1)}, u32[]{:S(2)}, u32[]{:S(2)}) collective-permute-start(bf16[768,768]{1,0:T(8,128)(2,1)} %refs_4_.7), channel_id=1, source_target_pairs={{0,1},{1,0},{2,3},{3,2},{4,5},{5,4},{6,7},{7,6},{8,9},{9,8},{10,11... | collective-permute-start | bytes 3538952 | tf_op jit(solution)/shard_map/ppermute | solution.py:1096
  43.4 32.1 %collective-permute-start.6 = (bf16[768,768]{1,0:T(8,128)(2,1)}, bf16[768,768]{1,0:T(8,128)(2,1)}, u32[]{:S(2)}, u32[]{:S(2)}) collective-permute-start(bf16[768,768]{1,0:T(8,128)(2,1)} %refs_5_.5), channel_id=1, source_target_pairs={{0,1},{1,0},{2,3},{3,2},{4,5},{5,4},{6,7},{7,6},{8,9},{9,8},{10,11... | collective-permute-start | bytes 3538952 | tf_op jit(solution)/shard_map/ppermute | solution.py:1096
  48.4 28.6 %collective-permute-start.2 = (bf16[2,416,768]{2,1,0:T(8,128)(2,1)}, bf16[2,416,768]{2,1,0:T(8,128)(2,1)S(1)}, u32[]{:S(2)}, u32[]{:S(2)}) collective-permute-start(bf16[2,416,768]{2,1,0:T(8,128)(2,1)} %all-gather.4.cloned.1.call-done.refs_0_.refs_2_.refs_4_.refs_6_), channel_id=1, source_target_pairs={{0,1},{1,0},{2,3},{3,2},{4,5},{5,4},{6,7},{7,6},{8,9},{9,8},{10,11... | collective-permute-start | bytes 3833864 | tf_op jit(solution)/shard_map/ppermute | solution.py:1096
  52.3 23.2 %collective-permute-start.3 = (bf16[384,768]{1,0:T(8,128)(2,1)}, bf16[384,768]{1,0:T(8,128)(2,1)}, u32[]{:S(2)}, u32[]{:S(2)}) collective-permute-start(bf16[384,768]{1,0:T(8,128)(2,1)} %constant_dynamic-slice_fusion.1), channel_id=1, source_target_pairs={{0,2},{1,3},{2,0},{3,1},{4,6},{5,7},{6,4},{7,5},{8,10},{9,11},{10,... | collective-permute-start | bytes 1769480 | tf_op jit(solution)/shard_map/ppermute | solution.py:1099
  54.1 21.4 %collective-permute-start.4 = (bf16[256,768]{1,0:T(8,128)(2,1)}, bf16[256,768]{1,0:T(8,128)(2,1)}, u32[]{:S(2)}, u32[]{:S(2)}) collective-permute-start(bf16[256,768]{1,0:T(8,128)(2,1)} %get-tuple-element.119.refs_0_.refs_8_), channel_id=1, source_target_pairs={{0,1},{1,0},{2,3},{3,2},{4,5},{5,4},{6,7},{7,6},{8,9},{9,8},{10,11... | collective-permute-start | bytes 1179656 | tf_op jit(solution)/shard_map/ppermute | solution.py:1096
  75.5 27.2 %collective-permute-start.9 = (bf16[384,768]{1,0:T(8,128)(2,1)}, bf16[384,768]{1,0:T(8,128)(2,1)}, u32[]{:S(2)}, u32[]{:S(2)}) collective-permute-start(bf16[384,768]{1,0:T(8,128)(2,1)} %collective-permute-done.3.refs_14_), channel_id=1, source_target_pairs={{0,4},{4,0},{8,12},{12,8},{16,20},{20,16},{24,28},{28,24},{1,5},{5... | collective-permute-start | bytes 1769480 | tf_op jit(solution)/shard_map/ppermute | solution.py:1113
  95.8 20.3 %copy-start.39 = (f32[1,768]{1,0:T(1,128)S(1)}, f32[1,768]{1,0:T(1,128)}, u32[]{:S(2)}) copy-start(f32[1,768]{1,0:T(1,128)} %reshape.56.refs_4_.refs_9_.refs_6_) | copy-start | bytes 9220
  95.8 2.7 %collective-permute-start.7 = (bf16[256,768]{1,0:T(8,128)(2,1)}, bf16[256,768]{1,0:T(8,128)(2,1)}, u32[]{:S(2)}, u32[]{:S(2)}) collective-permute-start(bf16[256,768]{1,0:T(8,128)(2,1)} %copy-done.42), channel_id=1, source_target_pairs={{0,1},{1,0},{2,3},{3,2},{4,5},{5,4},{6,7},{7,6},{8,9},{9,8},{10,11... | collective-permute-start | bytes 1179656 | tf_op jit(solution)/shard_map/ppermute | solution.py:1096
  97.8 16.0 %collective-permute-start.12 = (bf16[384,768]{1,0:T(8,128)(2,1)}, bf16[384,768]{1,0:T(8,128)(2,1)}, u32[]{:S(2)}, u32[]{:S(2)}) collective-permute-start(bf16[384,768]{1,0:T(8,128)(2,1)} %dynamic-slice_bitcast_fusion.refs_20_), channel_id=1, source_target_pairs={{0,4},{4,0},{8,12},{12,8},{16,20},{20,16},{24,28},{28,24},{1,5},{5... | collective-permute-start | bytes 1769480 | tf_op jit(solution)/shard_map/ppermute | solution.py:1113
  99.6 14.2 %collective-permute-start.8 = (bf16[128,768]{1,0:T(8,128)(2,1)S(1)}, bf16[128,768]{1,0:T(8,128)(2,1)S(1)}, u32[]{:S(2)}, u32[]{:S(2)}) collective-permute-start(bf16[128,768]{1,0:T(8,128)(2,1)S(1)} %add_convert_fusion.4), channel_id=1, source_target_pairs={{0,2},{1,3},{2,0},{3,1},{4,6},{5,7},{6,4},{7,5},{8,10},{9,11},{10,... | collective-permute-start | bytes 589832 | tf_op jit(solution)/shard_map/ppermute | solution.py:1099
  102.2 11.7 %collective-permute-start.10 = (bf16[384,768]{1,0:T(8,128)(2,1)}, bf16[384,768]{1,0:T(8,128)(2,1)S(1)}, u32[]{:S(2)}, u32[]{:S(2)}) collective-permute-start(bf16[384,768]{1,0:T(8,128)(2,1)} %collective-permute-done.3.refs_14_), channel_id=1, source_target_pairs={{0,1},{1,0},{2,3},{3,2},{4,5},{5,4},{6,7},{7,6},{8,9},{9,8},{10,11... | collective-permute-start | bytes 1769480 | tf_op jit(solution)/shard_map/ppermute | solution.py:1096
  102.2 11.7 %collective-permute-start.13 = (bf16[384,768]{1,0:T(8,128)(2,1)}, bf16[384,768]{1,0:T(8,128)(2,1)S(1)}, u32[]{:S(2)}, u32[]{:S(2)}) collective-permute-start(bf16[384,768]{1,0:T(8,128)(2,1)} %dynamic-slice_bitcast_fusion.refs_20_), channel_id=1, source_target_pairs={{0,1},{1,0},{2,3},{3,2},{4,5},{5,4},{6,7},{7,6},{8,9},{9,8},{10,11... | collective-permute-start | bytes 1769480 | tf_op jit(solution)/shard_map/ppermute | solution.py:1096
  102.7 11.2 %collective-permute-start.11 = (bf16[384,768]{1,0:T(8,128)(2,1)}, bf16[384,768]{1,0:T(8,128)(2,1)S(1)}, u32[]{:S(2)}, u32[]{:S(2)}) collective-permute-start(bf16[384,768]{1,0:T(8,128)(2,1)} %collective-permute-done.9.refs_15_), channel_id=1, source_target_pairs={{0,1},{1,0},{2,3},{3,2},{4,5},{5,4},{6,7},{7,6},{8,9},{9,8},{10,11... | collective-permute-start | bytes 1769480 | tf_op jit(solution)/shard_map/ppermute | solution.py:1096
  113.9 2.2 collective-permute-start.14
  116.1 24.8 %slice-start = ((s8[5111808]{0:T(1024)(128)(4,1)}), s8[4194304]{0:T(1024)(128)(4,1)S(1)}, s32[]{:S(2)}) async-start(s8[5111808]{0:T(1024)(128)(4,1)} %bitcast.31), calls=%async_computation.2 | async-start | bytes 8388608
  120.8 20.2 %copy-start.12 = (bf16[3,1664,128]{2,1,0:T(8,128)(2,1)S(1)}, bf16[3,1664,128]{2,1,0:T(8,128)(2,1)}, u32[]{:S(2)}) copy-start(bf16[3,1664,128]{2,1,0:T(8,128)(2,1)} %copy-done.11) | copy-start | bytes 3833860
  120.8 20.2 %copy-start.22 = (bf16[192,768]{1,0:T(8,128)(2,1)S(1)}, bf16[192,768]{1,0:T(8,128)(2,1)}, u32[]{:S(2)}) copy-start(bf16[192,768]{1,0:T(8,128)(2,1)} %refs_4_.6) | copy-start | bytes 884740
  120.8 20.2 %copy-start.31 = (f32[3,512,128]{2,1,0:T(8,128)S(1)}, f32[3,512,128]{2,1,0:T(8,128)}, u32[]{:S(2)}) copy-start(f32[3,512,128]{2,1,0:T(8,128)} %copy-done.30) | copy-start | bytes 2359300
  120.8 20.2 %copy-start.37 = (bf16[512,192]{1,0:T(8,128)(2,1)S(1)}, bf16[512,192]{1,0:T(8,128)(2,1)}, u32[]{:S(2)}) copy-start(bf16[512,192]{1,0:T(8,128)(2,1)} %copy-done.36) | copy-start | bytes 589828
  131.5 7.7 %collective-permute-start.15 = (bf16[128,768]{1,0:T(8,128)(2,1)S(1)}, bf16[128,768]{1,0:T(8,128)(2,1)S(1)}, u32[]{:S(2)}, u32[]{:S(2)}) collective-permute-start(bf16[128,768]{1,0:T(8,128)(2,1)S(1)} %get-tuple-element.139.refs_0_), channel_id=1, source_target_pairs={{0,2},{1,3},{2,0},{3,1},{4,6},{5,7},{6,4},{7,5},{8,10},{9,11},{10,... | collective-permute-start | bytes 589832 | tf_op jit(solution)/shard_map/ppermute | solution.py:1099
  134.0 6.9 %collective-permute-start.16 = (bf16[128,768]{1,0:T(8,128)(2,1)S(1)}, bf16[128,768]{1,0:T(8,128)(2,1)S(1)}, u32[]{:S(2)}, u32[]{:S(2)}) collective-permute-start(bf16[128,768]{1,0:T(8,128)(2,1)S(1)} %get-tuple-element.139.refs_0_), channel_id=1, source_target_pairs={{0,1},{1,0},{2,3},{3,2},{4,5},{5,4},{6,7},{7,6},{8,9},{9,8},{10,11... | collective-permute-start | bytes 589832 | tf_op jit(solution)/shard_map/ppermute | solution.py:1096
  139.2 1.8 collective-permute-start.17
  139.2 12.8 %collective-permute-start.21 = (bf16[2,128,768]{2,1,0:T(8,128)(2,1)S(1)}, bf16[2,128,768]{2,1,0:T(8,128)(2,1)S(1)}, u32[]{:S(2)}, u32[]{:S(2)}) collective-permute-start(bf16[2,128,768]{2,1,0:T(8,128)(2,1)S(1)} %get-tuple-element.147.refs_0_), channel_id=1, source_target_pairs={{0,2},{1,3},{2,0},{3,1},{4,6},{5,7},{6,4},{7,5},{8,10},{9,11},{10,... | collective-permute-start | bytes 1179656 | tf_op jit(solution)/shard_map/ppermute | solution.py:1099
  151.4 1.8 collective-permute-start.18
  151.7 3.1 %collective-permute-start.20 = (bf16[2,128,768]{2,1,0:T(8,128)(2,1)S(1)}, bf16[2,128,768]{2,1,0:T(8,128)(2,1)S(1)}, u32[]{:S(2)}, u32[]{:S(2)}) collective-permute-start(bf16[2,128,768]{2,1,0:T(8,128)(2,1)S(1)} %get-tuple-element.147.refs_0_), channel_id=1, source_target_pairs={{0,1},{1,0},{2,3},{3,2},{4,5},{5,4},{6,7},{7,6},{8,9},{9,8},{10,11... | collective-permute-start | bytes 1179656 | tf_op jit(solution)/shard_map/ppermute | solution.py:1096
  151.9 2.8 %collective-permute-start.22 = (bf16[2,128,768]{2,1,0:T(8,128)(2,1)S(1)}, bf16[2,128,768]{2,1,0:T(8,128)(2,1)S(1)}, u32[]{:S(2)}, u32[]{:S(2)}) collective-permute-start(bf16[2,128,768]{2,1,0:T(8,128)(2,1)S(1)} %collective-permute-done.21.refs_2_), channel_id=1, source_target_pairs={{0,1},{1,0},{2,3},{3,2},{4,5},{5,4},{6,7},{7,6},{8,9},{9,8},{10,11... | collective-permute-start | bytes 1179656 | tf_op jit(solution)/shard_map/ppermute | solution.py:1096
  153.2 11.3 %collective-permute-start.19 = (bf16[256,768]{1,0:T(8,128)(2,1)S(1)}, bf16[256,768]{1,0:T(8,128)(2,1)S(1)}, u32[]{:S(2)}, u32[]{:S(2)}) collective-permute-start(bf16[256,768]{1,0:T(8,128)(2,1)S(1)} %add_convert_fusion.2.refs_2_), channel_id=1, source_target_pairs={{0,2},{1,3},{2,0},{3,1},{4,6},{5,7},{6,4},{7,5},{8,10},{9,11},{10,... | collective-permute-start | bytes 1179656 | tf_op jit(solution)/shard_map/ppermute | solution.py:1099
  166.0 4.4 %collective-permute-start.23 = (bf16[256,768]{1,0:T(8,128)(2,1)S(1)}, bf16[256,768]{1,0:T(8,128)(2,1)S(1)}, u32[]{:S(2)}, u32[]{:S(2)}) collective-permute-start(bf16[256,768]{1,0:T(8,128)(2,1)S(1)} %get-tuple-element.151.refs_13_.refs_0_), channel_id=1, source_target_pairs={{0,1},{1,0},{2,3},{3,2},{4,5},{5,4},{6,7},{7,6},{8,9},{9,8},{10,11... | collective-permute-start | bytes 1179656 | tf_op jit(solution)/shard_map/ppermute | solution.py:1096
  168.1 35.8 %collective-permute-start.27 = (bf16[2,416,768]{2,1,0:T(8,128)(2,1)S(1)}, bf16[2,416,768]{2,1,0:T(8,128)(2,1)S(1)}, u32[]{:S(2)}, u32[]{:S(2)}) collective-permute-start(bf16[2,416,768]{2,1,0:T(8,128)(2,1)S(1)} %get-tuple-element.154), channel_id=1, source_target_pairs={{0,1},{1,0},{2,3},{3,2},{4,5},{5,4},{6,7},{7,6},{8,9},{9,8},{10,11... | collective-permute-start | bytes 3833864 | tf_op jit(solution)/shard_map/ppermute | solution.py:1096
  168.7 28.0 %collective-permute-start.29 = (bf16[384,1536]{1,0:T(8,128)(2,1)S(1)}, bf16[384,1536]{1,0:T(8,128)(2,1)S(1)}, u32[]{:S(2)}, u32[]{:S(2)}) collective-permute-start(bf16[384,1536]{1,0:T(8,128)(2,1)S(1)} %get-tuple-element.174), channel_id=1, source_target_pairs={{0,8},{4,12},{8,0},{12,4},{16,24},{20,28},{24,16},{28,20},{1,9},{5... | collective-permute-start | bytes 3538952 | tf_op jit(solution)/shard_map/ppermute | solution.py:1113
  180.1 2.1 collective-permute-start.24
  180.2 22.5 %collective-permute-start.30 = (bf16[432,960]{1,0:T(8,128)(2,1)S(1)}, bf16[432,960]{1,0:T(8,128)(2,1)S(1)}, u32[]{:S(2)}, u32[]{:S(2)}) collective-permute-start(bf16[432,960]{1,0:T(8,128)(2,1)S(1)} %get-tuple-element.178), channel_id=1, source_target_pairs={{0,4},{4,0},{8,12},{12,8},{16,20},{20,16},{24,28},{28,24},{1,5},{5... | collective-permute-start | bytes 2488328 | tf_op jit(solution)/shard_map/ppermute | solution.py:1113
  182.3 54.6 %collective-permute-start.25 = (bf16[512,768]{1,0:T(8,128)(2,1)S(1)}, bf16[512,768]{1,0:T(8,128)(2,1)S(1)}, u32[]{:S(2)}, u32[]{:S(2)}) collective-permute-start(bf16[512,768]{1,0:T(8,128)(2,1)S(1)} %pad_maximum_fusion), channel_id=1, source_target_pairs={{0,2},{1,3},{2,0},{3,1},{4,6},{5,7},{6,4},{7,5},{8,10},{9,11},{10,... | collective-permute-start | bytes 2359304 | tf_op jit(solution)/shard_map/ppermute | solution.py:1099
  183.7 30.4 %collective-permute-start.31 = (bf16[432,576]{1,0:T(8,128)(2,1)S(1)}, bf16[432,576]{1,0:T(8,128)(2,1)S(1)}, u32[]{:S(2)}, u32[]{:S(2)}) collective-permute-start(bf16[432,576]{1,0:T(8,128)(2,1)S(1)} %get-tuple-element.182), channel_id=1, source_target_pairs={{0,4},{4,0},{8,12},{12,8},{16,20},{20,16},{24,28},{28,24},{1,5},{5... | collective-permute-start | bytes 1493000 | tf_op jit(solution)/shard_map/ppermute | solution.py:1113
  197.4 28.3 %collective-permute-start.32 = (bf16[192,1536]{1,0:T(8,128)(2,1)S(1)}, bf16[192,1536]{1,0:T(8,128)(2,1)S(1)}, u32[]{:S(2)}, u32[]{:S(2)}) collective-permute-start(bf16[192,1536]{1,0:T(8,128)(2,1)S(1)} %get-tuple-element.175), channel_id=1, source_target_pairs={{0,16},{4,20},{8,24},{12,28},{16,0},{20,4},{24,8},{28,12},{1,17},{... | collective-permute-start | bytes 1769480 | tf_op jit(solution)/shard_map/ppermute | solution.py:1113
  203.5 25.3 %collective-permute-start.33 = (bf16[240,960]{1,0:T(8,128)(2,1)S(1)}, bf16[240,960]{1,0:T(8,128)(2,1)S(1)}, u32[]{:S(2)}, u32[]{:S(2)}) collective-permute-start(bf16[240,960]{1,0:T(8,128)(2,1)S(1)} %get-tuple-element.179), channel_id=1, source_target_pairs={{0,8},{4,12},{8,0},{12,4},{16,24},{20,28},{24,16},{28,20},{1,9},{5... | collective-permute-start | bytes 1382408 | tf_op jit(solution)/shard_map/ppermute | solution.py:1113
  204.0 36.1 %collective-permute-start.28 = (bf16[416,768]{1,0:T(8,128)(2,1)S(1)}, bf16[416,768]{1,0:T(8,128)(2,1)S(1)}, u32[]{:S(2)}, u32[]{:S(2)}) collective-permute-start(bf16[416,768]{1,0:T(8,128)(2,1)S(1)} %fusion.1), channel_id=1, source_target_pairs={{0,2},{1,3},{2,0},{3,1},{4,6},{5,7},{6,4},{7,5},{8,10},{9,11},{10,... | collective-permute-start | bytes 1916936 | tf_op jit(solution)/shard_map/ppermute | solution.py:1099
  214.8 21.0 %collective-permute-start.34 = (bf16[240,576]{1,0:T(8,128)(2,1)S(1)}, bf16[240,576]{1,0:T(8,128)(2,1)S(1)}, u32[]{:S(2)}, u32[]{:S(2)}) collective-permute-start(bf16[240,576]{1,0:T(8,128)(2,1)S(1)} %get-tuple-element.183), channel_id=1, source_target_pairs={{0,8},{4,12},{8,0},{12,4},{16,24},{20,28},{24,16},{28,20},{1,9},{5... | collective-permute-start | bytes 829448 | tf_op jit(solution)/shard_map/ppermute | solution.py:1113
  226.5 12.3 %collective-permute-start.35 = (bf16[96,1536]{1,0:T(8,128)(2,1)S(1)}, bf16[96,1536]{1,0:T(8,128)(2,1)S(1)}, u32[]{:S(2)}, u32[]{:S(2)}) collective-permute-start(bf16[96,1536]{1,0:T(8,128)(2,1)S(1)} %get-tuple-element.186), channel_id=1, source_target_pairs={{0,4},{4,0},{8,12},{12,8},{16,20},{20,16},{24,28},{28,24},{1,5},{5... | collective-permute-start | bytes 884744 | tf_op jit(solution)/shard_map/ppermute | solution.py:1113
  229.5 19.1 %collective-permute-start.36 = (bf16[144,960]{1,0:T(8,128)(2,1)S(1)}, bf16[144,960]{1,0:T(8,128)(2,1)S(1)}, u32[]{:S(2)}, u32[]{:S(2)}) collective-permute-start(bf16[144,960]{1,0:T(8,128)(2,1)S(1)} %get-tuple-element.190), channel_id=1, source_target_pairs={{0,16},{4,20},{8,24},{12,28},{16,0},{20,4},{24,8},{28,12},{1,17},{... | collective-permute-start | bytes 829448 | tf_op jit(solution)/shard_map/ppermute | solution.py:1113
  236.4 14.3 %collective-permute-start.37 = (bf16[144,576]{1,0:T(8,128)(2,1)S(1)}, bf16[144,576]{1,0:T(8,128)(2,1)S(1)}, u32[]{:S(2)}, u32[]{:S(2)}) collective-permute-start(bf16[144,576]{1,0:T(8,128)(2,1)S(1)} %get-tuple-element.194), channel_id=1, source_target_pairs={{0,16},{4,20},{8,24},{12,28},{16,0},{20,4},{24,8},{28,12},{1,17},{... | collective-permute-start | bytes 497672 | tf_op jit(solution)/shard_map/ppermute | solution.py:1113
  237.1 20.5 %collective-permute-start.26 = (f32[256,768]{1,0:T(8,128)S(1)}, f32[256,768]{1,0:T(8,128)S(1)}, u32[]{:S(2)}, u32[]{:S(2)}) collective-permute-start(f32[256,768]{1,0:T(8,128)S(1)} %add_add_fusion.refs_0_), channel_id=1, source_target_pairs={{0,1},{1,0},{2,3},{3,2},{4,5},{5,4},{6,7},{7,6},{8,9},{9,8},{10,11... | collective-permute-start | bytes 2359304 | tf_op jit(solution)/shard_map/ppermute | solution.py:1096
  250.0 2.1 collective-permute-start.38
  252.1 4.2 %collective-permute-start.39 = (f32[16,768]{1,0:T(8,128)S(1)}, f32[16,768]{1,0:T(8,128)S(1)}, u32[]{:S(2)}, u32[]{:S(2)}) collective-permute-start(f32[16,768]{1,0:T(8,128)S(1)} %add.81), channel_id=1, source_target_pairs={{0,2},{1,3},{2,0},{3,1},{4,6},{5,7},{6,4},{7,5},{8,10},{9,11},{10,... | collective-permute-start | bytes 147464 | tf_op jit(solution)/shard_map/ppermute | solution.py:1053
  (42 other events, 261.4 us)
Sparse Core Ops, SparseCore 0:
  18.0 30.3 all-gather.3
  50.5 30.5 all-gather.5
